TPU v7x, 256 devices: a whole 4x4x8 slice. The times are simulated.
256 devices in a mesh: dp: 8 (over z_lo, x), ctx: 32 (over z_hi, y, core).
Axes of the slice: x: 4, y: 4, z: 8 (z_hi: 4, z_lo: 2; z = z_hi * 2 + z_lo), core: 2. Of those that a mesh axis runs over, the one named last changes fastest.
Arguments:
- queries: bfloat16 [8, 4096, 2048], P('dp', 'ctx'), may hold values from -6 to 6
- keys: bfloat16 [8, 4096, 2048], P('dp', 'ctx'), may hold values from -6 to 6
- values: bfloat16 [8, 4096, 2048], P('dp', 'ctx'), may hold values from -6 to 6
- upstream: bfloat16 [8, 4096, 2048], P('dp', 'ctx'), may hold values from -6 to 6
- filters: float32 [2048, 4096], P('ctx'), may hold values from -0.09375 to 0.09375
- out_weight: bfloat16 [2048, 2048], P('ctx'), may hold values from -0.125 to 0.125
Outputs:
- grad_queries: bfloat16 [8, 4096, 2048], P('dp', 'ctx')
- grad_keys: bfloat16 [8, 4096, 2048], P('dp', 'ctx')
- grad_values: bfloat16 [8, 4096, 2048], P('dp', 'ctx')
- grad_filters: float32 [2048, 4096], P('ctx')
- grad_weight: float32 [2048, 2048], P('ctx')
All inputs are finite; a program needn't handle non-finite values.
Results may differ from a plain program's by a relative error of at most 0.019.
Values may be sent and summed in bfloat16 or wider, within the bound.
A program may use at most 128 MiB of HBM per device.

v0:
```python
import functools
import math

import jax
import jax.numpy as jnp
import numpy as np
from jax import lax
from jax.experimental import pallas as pl
from jax.experimental.pallas import tpu as pltpu
from jax.sharding import PartitionSpec as P

NX, NZL, NZH, NY, NC = 4, 2, 4, 4, 2
TOK, CH = 128, 64
BF, F32 = jnp.bfloat16, jnp.float32
MESH = pl.DeviceIdType.MESH


def place():
    dp = lax.axis_index("dp")
    ctx = lax.axis_index("ctx")
    near = NY * NC
    return dict(
        dp=dp,
        ctx=ctx,
        x=lax.rem(dp, NX),
        zl=dp // NX,
        zh=ctx // near,
        near=lax.rem(ctx, near),
        y=lax.rem(ctx, near) // NC,
        core=lax.rem(ctx, NC),
    )


def send(src, dst, ssem, rsem, dp, ctx):
    return pltpu.make_async_remote_copy(
        src_ref=src,
        dst_ref=dst,
        send_sem=ssem,
        recv_sem=rsem,
        device_id=(dp, ctx),
        device_id_type=MESH,
    )


R2 = math.sqrt(0.5)


def add(a, b):
    return tuple(p if q is None else q if p is None else p + q for p, q in zip(a, b))


def neg(a):
    return tuple(None if p is None else -p for p in a)


def sub(a, b):
    return tuple(
        p if q is None else -q if p is None else p - q for p, q in zip(a, b)
    )


def conj(a):
    return (a[0], None if a[1] is None else -a[1])


def turn(a):
    return (None if a[1] is None else -a[1], a[0])


def unturn(a):
    return (a[1], None if a[0] is None else -a[0])


def times(a, angle):
    c, s = math.cos(angle), math.sin(angle)
    if a[1] is None:
        return (a[0] * c, a[0] * s)
    return (a[0] * c - a[1] * s, a[0] * s + a[1] * c)


def fft4(a, b, c, d, sign):
    s0, s1, s2, s3 = add(a, c), sub(a, c), add(b, d), sub(b, d)
    t3 = turn(s3) if sign > 0 else unturn(s3)
    return [add(s0, s2), add(s1, t3), sub(s0, s2), sub(s1, t3)]


def eighth(a, sign):
    if a[1] is None:
        return (a[0] * R2, a[0] * (R2 * sign))
    if sign > 0:
        return ((a[0] - a[1]) * R2, (a[0] + a[1]) * R2)
    return ((a[0] + a[1]) * R2, (a[1] - a[0]) * R2)


def fft8(v, sign):
    even = fft4(v[0], v[2], v[4], v[6], sign)
    odd = fft4(v[1], v[3], v[5], v[7], sign)
    quarter = turn if sign > 0 else unturn
    odd = [odd[0], eighth(odd[1], sign), quarter(odd[2]), quarter(eighth(odd[3], sign))]
    return [add(e, o) for e, o in zip(even, odd)] + [sub(e, o) for e, o in zip(even, odd)]


def split_rows(x):
    a = [[None] * 8 for _ in range(5)]
    for j in range(8):
        x0, x1, x2, x3 = x[j], x[8 + j], x[16 + j], x[24 + j]
        d, e = (x1 - x3) * R2, (x1 + x3) * R2
        s02, s13 = x0 + x2, x1 + x3
        a[0][j] = (s02 + s13, None)
        a[4][j] = (s02 - s13, None)
        a[2][j] = (x0 - x2, x3 - x1)
        a[1][j] = (x0 + d, -(x2 + e))
        a[3][j] = (x0 - d, x2 - e)
    out = [None] * 33
    for p in range(5):
        b = [a[p][j] if p * j == 0 else times(a[p][j], -2.0 * math.pi * p * j / 64) for j in range(8)]
        f = fft8(b, -1)
        for q in range(8):
            k = p + 8 * q
            if k <= 32:
                out[k] = f[q]
            elif 1 <= p <= 3:
                out[64 - k] = conj(f[q])
    return out


def join_rows(q):
    y = [None] * 32
    b = []
    for p in range(5):
        v = [q[p + 8 * i] if p + 8 * i <= 32 else conj(q[64 - p - 8 * i]) for i in range(8)]
        f = fft8(v, 1)
        b.append([f[j] if p * j == 0 else times(f[j], 2.0 * math.pi * p * j / 64) for j in range(8)])
    for j in range(8):
        b0, b4 = b[0][j][0], b[4][j][0]
        even, odd = 0.5 * (b0 + b4), 0.5 * (b0 - b4)
        (r1, i1), (r2, i2), (r3, i3) = b[1][j], b[2][j], b[3][j]
        y[j] = even + r2 + (r1 + r3)
        y[16 + j] = even - r2 + (i3 - i1)
        u, w = R2 * (r1 - r3), R2 * (i1 + i3)
        y[8 + j] = odd - i2 + (u - w)
        y[24 + j] = odd + i2 - (u + w)
    return y


def mixer_kernel(
    key_ref, value_ref, query_ref, up_ref, filt_ref, w_ref,
    cos_ref, sin_ref, wc_ref, ws_ref, wct_ref, wst_ref,
    gq_out, back_out, fg_out, gw_out,
    k_own, v_own, q_own, f_own, mix_t, q_t, mix_all, q_all, up_all, w_all, gg_all, sc_all, scl_all,
    ft, it, tab, part, filt_s, mix_s, iq, conv_own, conv_all, back_own, fg_own, gate, gq_all,
    fg_x, fg_half, fg_z, fg_fin, gw_part, gw_x, gw_mid, gw_z, gw_fin,
    m_send, m_recv, u_send, u_recv, r_send, r_recv, p_send, p_recv, q_send, q_recv,
    w_send, w_recv, v_send, v_recv, s_send, s_recv, c_send, c_recv, b_send, b_recv,
    fx_send, fx_recv, fz_send, fz_recv, fa_send, fa_recv,
    g_send, g_recv, wx_send, wx_recv, wz_send, wz_recv, wa_send, wa_recv, local,
):
    at = place()
    dp, ctx, near, zh, zl, x = (at[k] for k in ("dp", "ctx", "near", "zh", "zl", "x"))
    y, core = at["y"], at["core"]
    nctx, nnear, ndp, nz = NZH * NY * NC, NY * NC, NX * NZL, NZH * NZL
    rows = CH // NX
    depth = up_ref.shape[-1]
    seq = nctx * TOK
    span = seq // NZL
    wide, narrow = depth // NX, depth // NX // NZL
    half = TOK // 2

    peers = [(dp, lax.rem(ctx + s, nctx)) for s in range(1, nctx)]
    peers += [(lax.rem(dp + s, ndp), ctx) for s in range(1, ndp)]
    other = lax.rem(zl + 1, NZL) * NX + x
    if NZL > 1:
        peers += [(other, lax.rem(zh + s, NZH) * nnear + near) for s in range(1, NZH)]
    barrier = pltpu.get_barrier_semaphore()
    for d, c in peers:
        pl.semaphore_signal(barrier, inc=1, device_id=(d, c), device_id_type=MESH)
    loads = [
        pltpu.make_async_copy(key_ref, k_own, local.at[0]),
        pltpu.make_async_copy(value_ref, v_own, local.at[1]),
        pltpu.make_async_copy(query_ref, q_own, local.at[2]),
        pltpu.make_async_copy(filt_ref, f_own, local.at[3]),
        pltpu.make_async_copy(up_ref, up_all.at[near], local.at[4]),
        pltpu.make_async_copy(w_ref, w_all.at[zh], local.at[5]),
    ]
    for copy in loads:
        copy.start()
    loads[0].wait()
    loads[1].wait()

    def mix_block(j, carry):
        cols = pl.ds(pl.multiple_of(j * 2 * CH, 2 * CH), 2 * CH)
        mixed = (k_own[:, cols].astype(F32) * v_own[:, cols].astype(F32)).astype(BF)
        turned = mixed.astype(F32).T.astype(BF)
        mix_t[2 * j] = turned[0:CH]
        mix_t[2 * j + 1] = turned[CH : 2 * CH]
        return carry

    lax.fori_loop(0, nctx // 2, mix_block, 0)
    mix_all[ctx] = mix_t[ctx]
    pl.semaphore_wait(barrier, len(peers))

    ms = []
    for s in range(1, nctx):
        to = lax.rem(ctx + s, nctx)
        ms.append(send(mix_t.at[to], mix_all.at[ctx], m_send.at[s], m_recv.at[s], dp, to))
        ms[-1].start()
    mine = pl.ds(pl.multiple_of(x * rows, rows), rows)
    ws = []
    for s in range(1, NZH):
        there = lax.rem(zh + s, NZH) * nnear + near
        ws.append(send(w_ref.at[mine], w_all.at[zh, mine], w_send.at[s], w_recv.at[s], dp, there))
        ws[-1].start()

    def along_y(step):
        return zh * nnear + lax.rem(y + step + NY, NY) * NC + core

    def slot_of(step, dc):
        return lax.rem(y + step + NY, NY) * NC + lax.rem(core + dc, NC)

    partner = zh * nnear + y * NC + lax.rem(core + 1, NC)
    steps = {4: (1, -1), 2: (1,), 1: ()}[NY]
    us = {}
    for order in range(2):
        for step in steps:
            h = order if step > 0 else 1 - order
            piece = pl.ds(h * half, half)
            i = (0 if step > 0 else 1) * 2 + h
            us[step, h] = send(
                up_ref.at[piece], up_all.at[near, piece], u_send.at[i], u_recv.at[i], dp, along_y(step)
            )
            us[step, h].start()
    pair = send(up_ref, up_all.at[near], p_send.at[0], p_recv.at[0], dp, partner)
    pair.start()

    loads[2].wait()

    def query_block(j, carry):
        cols = pl.ds(pl.multiple_of(j * 2 * CH, 2 * CH), 2 * CH)
        turned = q_own[:, cols].astype(F32).T.astype(BF)
        first = 2 * j
        q_t[lax.rem(first, nnear), first // nnear] = turned[0:CH]
        q_t[lax.rem(first + 1, nnear), (first + 1) // nnear] = turned[CH : 2 * CH]
        return carry

    lax.fori_loop(0, nctx // 2, query_block, 0)
    qs = []
    for s in range(1, nnear):
        to = lax.rem(near + s, nnear)
        qs.append(send(q_t.at[to], q_all.at[near], q_send.at[s], q_recv.at[s], dp, zh * nnear + to))
        qs[-1].start()
    q_all[near] = q_t[near]

    scale = 2.0 / 8192
    tab[0] = cos_ref[...]
    tab[1] = -sin_ref[...]
    tab[2] = cos_ref[...] * scale
    tab[3] = sin_ref[...] * scale

    def build(k, carry):
        a, b = tab[0], tab[1]
        ft[k, 0:128, 0:128] = a.astype(BF)
        ft[k, 128:256, 128:256] = a.astype(BF)
        ft[k, 0:128, 128:256] = b.astype(BF)
        ft[k, 128:256, 0:128] = (-b).astype(BF)
        c, s = wc_ref[...], ws_ref[...]
        tab[0] = a * c + b * s
        tab[1] = b * c - a * s
        a, b = tab[2], tab[3]
        it[k, 0:128, 0:128] = a.astype(BF)
        it[k, 128:256, 128:256] = a.astype(BF)
        it[k, 0:128, 128:256] = b.astype(BF)
        it[k, 128:256, 0:128] = (-b).astype(BF)
        c, s = wct_ref[...], wst_ref[...]
        tab[2] = a * c - b * s
        tab[3] = b * c + a * s
        return carry

    lax.fori_loop(0, 33, build, 0)

    def sections(source):
        def body(block, carry):
            at16 = pl.ds(pl.multiple_of(block * 16, 16), 16)
            for lo in (0, 8):
                to = pl.ds(pl.multiple_of(block * 16 + lo, 8), 8)
                if source is None:
                    v = [f_own[to, n * TOK : (n + 1) * TOK] for n in range(nctx)]
                else:
                    v = [source[n, at16].astype(F32)[lo : lo + 8] for n in range(nctx)]
                v += [jnp.zeros_like(v[0])] * (32 - nctx)
                for k, (re, im) in enumerate(split_rows(v)):
                    part[k, to, 0:128] = re
                    part[k, to, 128:256] = jnp.zeros_like(re) if im is None else im
            return carry

        lax.fori_loop(0, CH // 16, body, 0)

    def rejoin(lo_row, target):
        def body(block, carry):
            at16 = pl.ds(pl.multiple_of(block * 16, 16), 16)
            halves = []
            for lo in (0, 8):
                to = pl.ds(pl.multiple_of(lo_row + block * 16 + lo, 8), 8)
                halves.append(
                    join_rows([(iq[k, to, 0:128], iq[k, to, 128:256]) for k in range(33)])
                )
            for n in range(nctx):
                value = jnp.concatenate([halves[0][n], halves[1][n]], axis=0).astype(BF)
                if target is fg_own:
                    target[at16, n * TOK : (n + 1) * TOK] = value
                else:
                    target[n, at16] = value
            return carry

        lax.fori_loop(0, CH // 16, body, 0)

    def forward(k):
        full = jnp.dot(part[k].astype(BF), ft[k], preferred_element_type=F32)
        return full[:, 0:128], full[:, 128:256]

    loads[3].wait()
    sections(None)

    vs = []
    for s, copy in enumerate(ws, 1):
        copy.wait_recv()
        shard = lax.rem(zh + NZH - s, NZH)
        for t in range(1, NX):
            there = zl * NX + lax.rem(x + t, NX)
            piece = w_all.at[shard, mine]
            vs.append(send(piece, piece, v_send.at[s, t], v_recv.at[s, t], there, ctx))
            vs[-1].start()
    rs = []
    if NY == 4:
        for step, h in ((1, 0), (-1, 1)):
            us[step, h].wait_recv()
            piece = up_all.at[slot_of(-step, 0), pl.ds(h * half, half)]
            rs.append(send(piece, piece, r_send.at[h], r_recv.at[h], dp, along_y(step)))
            rs[-1].start()

    def filter_step(k, carry):
        re, im = forward(k)
        filt_s[k, :, 0:128] = re
        filt_s[k, :, 128:256] = im
        return carry

    lax.fori_loop(0, 33, filter_step, 0)

    relays = []

    def relay(slot, index):
        piece = up_all.at[slot]
        relays.append(send(piece, piece, p_send.at[index], p_recv.at[index], dp, partner))
        relays[-1].start()

    for i, step in enumerate(steps):
        for h in range(2):
            if not (NY == 4 and (step, h) in ((1, 0), (-1, 1))):
                us[step, h].wait_recv()
        relay(slot_of(-step, 0), 1 + i)

    for copy in ms:
        copy.wait_recv()
    sections(mix_all)

    def conv_step(k, carry):
        mr, mi = forward(k)
        mix_s[k, :, 0:128] = mr
        mix_s[k, :, 128:256] = mi
        fr, fi = filt_s[k, :, 0:128], filt_s[k, :, 128:256]
        both = jnp.concatenate([fr * mr - fi * mi, fr * mi + fi * mr], axis=1).astype(BF)
        iq[k, 0:CH] = jnp.dot(both, it[k], preferred_element_type=F32)
        return carry

    lax.fori_loop(0, 33, conv_step, 0)
    rejoin(0, conv_own)
    cs = []
    for s in range(1, NZH):
        to = lax.rem(zh + s, NZH)
        cs.append(
            send(
                conv_own.at[pl.ds(to * nnear, nnear)], conv_all.at[zh],
                c_send.at[s], c_recv.at[s], dp, to * nnear + near,
            )
        )
        cs[-1].start()
    for i in range(nnear):
        conv_all[zh, i] = conv_own[zh * nnear + i]

    far = slot_of(2, 0)
    if NY == 4:
        for copy in rs:
            copy.wait_recv()
        relay(far, 3)
    loads[4].wait()
    loads[5].wait()
    for copy in vs + qs:
        copy.wait_recv()
    ss = []

    def work(slot, k):
        w = w_all[...].reshape(NZH * CH, depth)
        gg = lax.dot_general(
            w, up_all[slot], (((1,), (1,)), ((), ())), preferred_element_type=F32
        ).astype(BF)
        gg = gg.reshape(NZH, CH, TOK)
        gg_all[slot] = gg
        sc_all[slot] = (gg.astype(F32) * q_all[slot].astype(F32)).astype(BF)
        n = zh * nnear + slot
        for s in range(1, NZH):
            to = lax.rem(zh + s, NZH)
            ss.append(
                send(
                    sc_all.at[slot, to], scl_all.at[n],
                    s_send.at[k, s], s_recv.at[k, s], dp, to * nnear + near,
                )
            )
            ss[-1].start()
        scl_all[n] = sc_all[slot, zh]

    work(near, 0)
    for i, step in enumerate(steps):
        work(slot_of(-step, 0), 1 + i)
    pair.wait_recv()
    work(slot_of(0, 1), NY)
    for i, step in enumerate(steps):
        relays[i].wait_recv()
        work(slot_of(-step, 1), NY + 1 + i)
    if NY == 4:
        work(far, 3)
        relays[2].wait_recv()
        work(slot_of(2, 1), 7)

    for copy in cs:
        copy.wait_recv()
    for i in range(nnear):
        for h in range(NZH):
            conv = conv_all[h, i].astype(F32)
            gq_all[i, h] = (gg_all[i, h].astype(F32) * conv).astype(BF)
            gate[h * CH : (h + 1) * CH, i * TOK : (i + 1) * TOK] = (
                q_all[i, h].astype(F32) * conv
            ).astype(BF)
    wxs = []
    for s in list(range(1, NX)) + [0]:
        to = lax.rem(x + s, NX)
        cols = pl.ds(pl.multiple_of(to * wide, wide), wide)
        up = up_all[:, :, cols].reshape(nnear * TOK, wide)
        gw_part[to] = jnp.dot(gate[...], up, preferred_element_type=F32).astype(BF)
        if s:
            wxs.append(
                send(gw_part.at[to], gw_x.at[x], wx_send.at[s], wx_recv.at[s], zl * NX + to, ctx)
            )
            wxs[-1].start()
    gw_x[x] = gw_part[x]
    gs = []
    for s in range(1, nnear):
        to = lax.rem(near + s, nnear)
        gs.append(
            send(gq_all.at[to], gq_out.at[:, near], g_send.at[s], g_recv.at[s], dp, zh * nnear + to)
        )
        gs[-1].start()
    own_g = pltpu.make_async_copy(gq_all.at[near], gq_out.at[:, near], local.at[7])
    own_g.start()

    for copy in ss:
        copy.wait_recv()
    sections(scl_all)

    def back_step(k, carry):
        gr, gi = forward(k)
        fr, fi = filt_s[k, :, 0:128], filt_s[k, :, 128:256]
        mr, mi = mix_s[k, :, 0:128], mix_s[k, :, 128:256]
        upper = jnp.concatenate([fr * gr + fi * gi, fr * gi - fi * gr], axis=1).astype(BF)
        lower = jnp.concatenate([mr * gr + mi * gi, mr * gi - mi * gr], axis=1).astype(BF)
        both = jnp.concatenate([upper, lower], axis=0)
        iq[k] = jnp.dot(both, it[k], preferred_element_type=F32)
        return carry

    lax.fori_loop(0, 33, back_step, 0)
    rejoin(0, back_own)
    bs = []
    for s in range(1, nctx):
        to = lax.rem(ctx + s, nctx)
        bs.append(send(back_own.at[to], back_out.at[ctx], b_send.at[s], b_recv.at[s], dp, to))
        bs[-1].start()
    own_b = pltpu.make_async_copy(back_own.at[ctx], back_out.at[ctx], local.at[8])
    own_b.start()
    rejoin(CH, fg_own)
    fxs = []
    for s in range(1, NX):
        to = lax.rem(x + s, NX)
        fxs.append(
            send(
                fg_own.at[pl.ds(pl.multiple_of(to * rows, rows), rows)], fg_x.at[x],
                fx_send.at[s], fx_recv.at[s], zl * NX + to, ctx,
            )
        )
        fxs[-1].start()
    fg_x[x] = fg_own[mine]

    for copy in wxs:
        copy.wait_recv()
    for h in range(NZH):
        total = gw_x[0, h * CH : (h + 1) * CH].astype(F32)
        for i in range(1, NX):
            total = total + gw_x[i, h * CH : (h + 1) * CH].astype(F32)
        for i in range(NZL):
            gw_mid[h, i] = total[:, i * narrow : (i + 1) * narrow].astype(BF)
    zs = []
    for s in range(NZH):
        for l in range(NZL):
            if s or l:
                to, tl = lax.rem(zh + s, NZH), lax.rem(zl + l, NZL)
                k = s * NZL + l
                zs.append(
                    send(
                        gw_mid.at[to, tl], gw_z.at[zh * NZL + zl],
                        wz_send.at[k], wz_recv.at[k], tl * NX + x, to * nnear + near,
                    )
                )
                zs[-1].start()
    gw_z[zh * NZL + zl] = gw_mid[zh, zl]

    for copy in fxs:
        copy.wait_recv()
    total = fg_x[0].astype(F32)
    for i in range(1, NX):
        total = total + fg_x[i].astype(F32)
    for i in range(NZL):
        fg_half[i] = total[:, i * span : (i + 1) * span].astype(BF)
    fzs = []
    for s in range(1, NZL):
        to = lax.rem(zl + s, NZL)
        fzs.append(
            send(fg_half.at[to], fg_z.at[zl], fz_send.at[s], fz_recv.at[s], to * NX + x, ctx)
        )
        fzs[-1].start()
    fg_z[zl] = fg_half[zl]

    for copy in zs:
        copy.wait_recv()
    total = gw_z[0].astype(F32)
    for i in range(1, nz):
        total = total + gw_z[i].astype(F32)
    gw_fin[...] = total.astype(BF)
    was = []
    wslot = gw_out.at[:, pl.ds(pl.multiple_of((x * NZL + zl) * narrow, narrow), narrow)]
    for s in range(1, ndp):
        to = lax.rem(dp + s, ndp)
        was.append(send(gw_fin, wslot, wa_send.at[s], wa_recv.at[s], to, ctx))
        was[-1].start()
    own_wa = pltpu.make_async_copy(gw_fin, wslot, local.at[9])
    own_wa.start()

    for copy in fzs:
        copy.wait_recv()
    total = fg_z[0].astype(F32)
    for i in range(1, NZL):
        total = total + fg_z[i].astype(F32)
    fg_fin[...] = total.astype(BF)
    fas = []
    fslot = fg_out.at[mine, pl.ds(pl.multiple_of(zl * span, span), span)]
    for s in range(1, ndp):
        to = lax.rem(dp + s, ndp)
        fas.append(send(fg_fin, fslot, fa_send.at[s], fa_recv.at[s], to, ctx))
        fas[-1].start()
    own_fa = pltpu.make_async_copy(fg_fin, fslot, local.at[10])
    own_fa.start()

    for copy in (own_g, own_b, own_wa, own_fa):
        copy.wait()
    sent = ms + ws + list(us.values()) + [pair] + qs + vs + rs + relays + cs + ss
    for copy in sent + wxs + fxs + fzs + zs:
        copy.wait_send()
    for copy in gs + bs + was + fas:
        copy.wait()


def mixer_call(keys, values, queries, up, filters, w):
    nctx, nnear, ndp, nz = NZH * NY * NC, NY * NC, NX * NZL, NZH * NZL
    depth = up.shape[-1]
    seq = nctx * TOK
    wide, narrow = depth // NX, depth // NX // NZL
    rows, span = CH // NX, seq // NZL
    i = np.arange(128)
    angle = 2.0 * np.pi * ((i[:, None] * i[None, :]) % 128) / 128
    step = np.broadcast_to((2.0 * np.pi * i / 8192)[:, None], (128, 128))
    tables = [np.cos(angle), np.sin(angle), np.cos(step), np.sin(step), np.cos(step.T), np.sin(step.T)]
    tables = [jnp.asarray(np.ascontiguousarray(t), F32) for t in tables]
    dma = pltpu.SemaphoreType.DMA
    hbm = pl.BlockSpec(memory_space=pl.ANY)
    vmem = pl.BlockSpec(memory_space=pltpu.VMEM)
    near4 = (nnear, NZH, CH, TOK)
    chans = (nctx, CH, TOK)
    spec = (33, CH, 256)
    pairs = [
        (nctx,), (4,), (2,), (4,), (nnear,), (NZH,), (NZH, NX), (nnear, NZH), (NZH,), (nctx,),
        (NX,), (NZL,), (ndp,), (nnear,), (NX,), (nz,), (ndp,),
    ]
    return pl.pallas_call(
        mixer_kernel,
        name="mixer",
        out_shape=[
            jax.ShapeDtypeStruct((NZH, nnear, CH, TOK), BF),
            jax.ShapeDtypeStruct(chans, BF),
            jax.ShapeDtypeStruct((CH, seq), BF),
            jax.ShapeDtypeStruct((CH, depth), BF),
        ],
        in_specs=[hbm] * 6 + [vmem] * 6,
        out_specs=[hbm] * 4,
        scratch_shapes=[
            pltpu.VMEM((TOK, nctx * CH), BF),
            pltpu.VMEM((TOK, nctx * CH), BF),
            pltpu.VMEM((TOK, nctx * CH), BF),
            pltpu.VMEM((CH, seq), F32),
            pltpu.VMEM(chans, BF),
            pltpu.VMEM(near4, BF),
            pltpu.VMEM(chans, BF),
            pltpu.VMEM(near4, BF),
            pltpu.VMEM((nnear, TOK, depth), BF),
            pltpu.VMEM((NZH, CH, depth), BF),
            pltpu.VMEM(near4, BF),
            pltpu.VMEM(near4, BF),
            pltpu.VMEM(chans, BF),
            pltpu.VMEM((33, 256, 256), BF),
            pltpu.VMEM((33, 256, 256), BF),
            pltpu.VMEM((4, 128, 128), F32),
            pltpu.VMEM(spec, F32),
            pltpu.VMEM(spec, F32),
            pltpu.VMEM(spec, F32),
            pltpu.VMEM((33, 2 * CH, 256), F32),
            pltpu.VMEM(chans, BF),
            pltpu.VMEM((NZH, nnear, CH, TOK), BF),
            pltpu.VMEM(chans, BF),
            pltpu.VMEM((CH, seq), BF),
            pltpu.VMEM((NZH * CH, nnear * TOK), BF),
            pltpu.VMEM(near4, BF),
            pltpu.VMEM((NX, rows, seq), BF),
            pltpu.VMEM((NZL, rows, span), BF),
            pltpu.VMEM((NZL, rows, span), BF),
            pltpu.VMEM((rows, span), BF),
            pltpu.VMEM((NX, NZH * CH, wide), BF),
            pltpu.VMEM((NX, NZH * CH, wide), BF),
            pltpu.VMEM((NZH, NZL, CH, narrow), BF),
            pltpu.VMEM((nz, CH, narrow), BF),
            pltpu.VMEM((CH, narrow), BF),
        ]
        + [dma(n) for n in pairs for _ in range(2)]
        + [dma((12,))],
        compiler_params=pltpu.CompilerParams(
            collective_id=0, has_side_effects=True, vmem_limit_bytes=60 << 20
        ),
    )(keys, values, queries, up, filters, w, *tables)


def per_device(queries, keys, values, upstream, filters, out_weight):
    nctx = NZH * NY * NC
    key_rows, value_rows = keys[0], values[0]
    gq, back, fg, gw = mixer_call(
        key_rows, value_rows, queries[0], upstream[0], filters, out_weight
    )
    grad_queries = gq.reshape(nctx * CH, TOK).T
    back_wide = back.reshape(nctx * CH, TOK).T.astype(F32)
    grad_keys = (back_wide * value_rows.astype(F32)).astype(BF)
    grad_values = (back_wide * key_rows.astype(F32)).astype(BF)
    return (grad_queries[None], grad_keys[None], grad_values[None], fg.astype(F32), gw.astype(F32))


def solution(mesh):
    rows = P("dp", "ctx", None)
    chans = P("ctx", None)
    return jax.shard_map(
        per_device,
        mesh=mesh,
        in_specs=(rows, rows, rows, rows, chans, chans),
        out_specs=(rows, rows, rows, chans, chans),
        check_vma=False,
    )
```

profile of v0, /device:TPU:1, one launch (start us, length us, event | category | flops | bytes accessed | tf_op | source)
XLA Modules:
  0.0 122.8 jit_solution(3983510285827687231)
XLA Ops:
  0.6 115.6 %mixer.1 = (bf16[4,8,64,128]{3,2,1,0:T(8,128)(2,1)}, bf16[32,64,128]{2,1,0:T(8,128)(2,1)}, bf16[64,4096]{1,0:T(8,128)(2,1)}, bf16[64,2048]{1,0:T(8,128)(2,1)}) custom-call(bf16[128,2048]{1,0:T(8,128)(2,1)} %bitcast.28, bf16[128,2048]{1,0:T(8,128)(2,1)} %bitcast.29, bf16[128,2048]{1,0:T(8,128)(2,1)} %bitcast.32, bf16[128,2048]{1,0:T(8,128)(2,1)} %bitcast.33, ...), custom_call_target="tpu_custom_call" | custom-call | tf_op jit(solution)/shard_map/mixer/pallas_call | solution.py:599
  116.2 1.1 bitcast_convert_fusion
  117.3 0.0 copy-start
  117.3 0.0 copy-start.1
  117.4 0.3 copy.20
  117.7 0.7 copy-done
  118.4 0.2 copy-done.1
  118.5 0.0 copy-start.2
  118.5 1.2 %fusion.2 = (bf16[1,128,2048]{2,1,0:T(8,128)(2,1)}, bf16[1,128,2048]{2,1,0:T(8,128)(2,1)}) fusion(f32[2048,128]{0,1:T(8,128)S(1)} %copy.20, bf16[1,128,2048]{2,1,0:T(8,128)(2,1)S(1)} %copy-done, bf16[1,128,2048]{2,1,0:T(8,128)(2,1)S(1)} %copy-done.1), kind=kLoop, calls=%fused_computation.4 | loop fusion | flops 1572864 | bytes 3145728 | tf_op jit(solution)/shard_map/broadcast_in_dim | solution.py:665
  119.8 0.0 copy-done.2
  119.8 0.0 copy-start.3
  119.8 1.0 convert_element_type.34
  120.8 0.2 copy-done.3
  121.0 0.0 copy-start.4
  121.0 1.0 copy.19
  122.0 0.0 copy-done.4
  122.0 0.8 convert_element_type.35
Async XLA Ops:
  117.3 1.0 copy-start
  117.3 1.2 copy-start.1
  118.5 1.2 %copy-start.2 = (bf16[64,4096]{1,0:T(8,128)(2,1)S(1)}, bf16[64,4096]{1,0:T(8,128)(2,1)}, u32[]{:S(2)}) copy-start(bf16[64,4096]{1,0:T(8,128)(2,1)} %get-tuple-element.11) | copy-start | bytes 1572868
  119.8 1.2 copy-start.3
  121.0 1.0 copy-start.4
where the time goes:
time: 124 us; the launch traced here: 123 us
  Pallas kernels  116 us (94%)
  other arithmetic  4.22 us (3%)
  local copies, waits for them, and re-layouts  2.36 us (2%)
    pallas_call x1, Pallas kernels, mixer_call(): pl.pallas_call(mixer_kernel, name='mixer', out_shape=[jax.ShapeDtypeStruc...  116 us

commit v1 on v0

--- a/solution.py
+++ b/solution.py
@@ -11,8 +11,14 @@
 
 NX, NZL, NZH, NY, NC = 4, 2, 4, 4, 2
 TOK, CH = 128, 64
+HALF = CH // 2
+UNROLL = 11
 BF, F32 = jnp.bfloat16, jnp.float32
 MESH = pl.DeviceIdType.MESH
+
+
+def drain(view, sem):
+    pltpu.make_async_copy(view, view, sem).wait()
 
 
 def place():
@@ -148,8 +154,8 @@
     cos_ref, sin_ref, wc_ref, ws_ref, wct_ref, wst_ref,
     gq_out, back_out, fg_out, gw_out,
     k_own, v_own, q_own, f_own, mix_t, q_t, mix_all, q_all, up_all, w_all, gg_all, sc_all, scl_all,
-    ft, it, tab, part, filt_s, mix_s, iq, conv_own, conv_all, back_own, fg_own, gate, gq_all,
-    fg_x, fg_half, fg_z, fg_fin, gw_part, gw_x, gw_mid, gw_z, gw_fin,
+    ft, it, tab, part, filt_s, mix_s, iq, conv_own, conv_all, back_own, fg_own, gate, gq_all, gq_in, back_in,
+    fg_x, fg_half, fg_z, fg_fin, gw_part, gw_x, gw_mid, gw_z, gw_fin, gw_sum,
     m_send, m_recv, u_send, u_recv, r_send, r_recv, p_send, p_recv, q_send, q_recv,
     w_send, w_recv, v_send, v_recv, s_send, s_recv, c_send, c_recv, b_send, b_recv,
     fx_send, fx_recv, fz_send, fz_recv, fa_send, fa_recv,
@@ -162,15 +168,26 @@
     rows = CH // NX
     depth = up_ref.shape[-1]
     seq = nctx * TOK
-    span = seq // NZL
     wide, narrow = depth // NX, depth // NX // NZL
     half = TOK // 2
 
-    peers = [(dp, lax.rem(ctx + s, nctx)) for s in range(1, nctx)]
-    peers += [(lax.rem(dp + s, ndp), ctx) for s in range(1, ndp)]
+    def ctx_order():
+        turns = sorted(range(NZH), key=lambda a: -min(a, NZH - a))
+        return [
+            lax.rem(zh + a, NZH) * nnear + lax.rem(near + b, nnear)
+            for a in turns
+            for b in range(nnear)
+            if a or b
+        ]
+
     other = lax.rem(zl + 1, NZL) * NX + x
+    peers = []
     if NZL > 1:
         peers += [(other, lax.rem(zh + s, NZH) * nnear + near) for s in range(1, NZH)]
+    peers += [(dp, to) for to in ctx_order()]
+    if NZL > 1:
+        peers += [(other, ctx)]
+    peers += [(zl * NX + lax.rem(x + s, NX), ctx) for s in range(1, NX)]
     barrier = pltpu.get_barrier_semaphore()
     for d, c in peers:
         pl.semaphore_signal(barrier, inc=1, device_id=(d, c), device_id_type=MESH)
@@ -200,15 +217,15 @@
     pl.semaphore_wait(barrier, len(peers))
 
     ms = []
-    for s in range(1, nctx):
-        to = lax.rem(ctx + s, nctx)
-        ms.append(send(mix_t.at[to], mix_all.at[ctx], m_send.at[s], m_recv.at[s], dp, to))
+    for s, to in enumerate(ctx_order(), 1):
+        ms.append(send(mix_t.at[to], mix_all.at[ctx], m_send.at[0], m_recv.at[0], dp, to))
         ms[-1].start()
+
     mine = pl.ds(pl.multiple_of(x * rows, rows), rows)
     ws = []
     for s in range(1, NZH):
         there = lax.rem(zh + s, NZH) * nnear + near
-        ws.append(send(w_ref.at[mine], w_all.at[zh, mine], w_send.at[s], w_recv.at[s], dp, there))
+        ws.append(send(w_ref.at[mine], w_all.at[zh, mine], w_send.at[0], w_recv.at[s], dp, there))
         ws[-1].start()
 
     def along_y(step):
@@ -226,7 +243,7 @@
             piece = pl.ds(h * half, half)
             i = (0 if step > 0 else 1) * 2 + h
             us[step, h] = send(
-                up_ref.at[piece], up_all.at[near, piece], u_send.at[i], u_recv.at[i], dp, along_y(step)
+                up_ref.at[piece], up_all.at[near, piece], u_send.at[0], u_recv.at[i], dp, along_y(step)
             )
             us[step, h].start()
     pair = send(up_ref, up_all.at[near], p_send.at[0], p_recv.at[0], dp, partner)
@@ -243,11 +260,16 @@
         return carry
 
     lax.fori_loop(0, nctx // 2, query_block, 0)
-    qs = []
-    for s in range(1, nnear):
-        to = lax.rem(near + s, nnear)
-        qs.append(send(q_t.at[to], q_all.at[near], q_send.at[s], q_recv.at[s], dp, zh * nnear + to))
-        qs[-1].start()
+    qs = {}
+    for dy in sorted(range(NY), key=lambda a: min(a, NY - a)):
+        for dc in range(NC):
+            if dy or dc:
+                to = slot_of(dy, dc)
+                s = dy * NC + dc
+                qs[dy, dc] = send(
+                    q_t.at[to], q_all.at[near], q_send.at[0], q_recv.at[s], dp, zh * nnear + to
+                )
+                qs[dy, dc].start()
     q_all[near] = q_t[near]
 
     scale = 2.0 / 8192
@@ -277,7 +299,7 @@
 
     lax.fori_loop(0, 33, build, 0)
 
-    def sections(source):
+    def sections(source, lo_block=0, blocks=CH // 16):
         def body(block, carry):
             at16 = pl.ds(pl.multiple_of(block * 16, 16), 16)
             for lo in (0, 8):
@@ -292,9 +314,9 @@
                     part[k, to, 128:256] = jnp.zeros_like(re) if im is None else im
             return carry
 
-        lax.fori_loop(0, CH // 16, body, 0)
-
-    def rejoin(lo_row, target):
+        lax.fori_loop(lo_block, lo_block + blocks, body, 0)
+
+    def rejoin(lo_row, target, lo_block=0, blocks=CH // 16):
         def body(block, carry):
             at16 = pl.ds(pl.multiple_of(block * 16, 16), 16)
             halves = []
@@ -311,7 +333,7 @@
                     target[n, at16] = value
             return carry
 
-        lax.fori_loop(0, CH // 16, body, 0)
+        lax.fori_loop(lo_block, lo_block + blocks, body, 0)
 
     def forward(k):
         full = jnp.dot(part[k].astype(BF), ft[k], preferred_element_type=F32)
@@ -320,21 +342,12 @@
     loads[3].wait()
     sections(None)
 
-    vs = []
-    for s, copy in enumerate(ws, 1):
-        copy.wait_recv()
-        shard = lax.rem(zh + NZH - s, NZH)
-        for t in range(1, NX):
-            there = zl * NX + lax.rem(x + t, NX)
-            piece = w_all.at[shard, mine]
-            vs.append(send(piece, piece, v_send.at[s, t], v_recv.at[s, t], there, ctx))
-            vs[-1].start()
     rs = []
     if NY == 4:
         for step, h in ((1, 0), (-1, 1)):
             us[step, h].wait_recv()
             piece = up_all.at[slot_of(-step, 0), pl.ds(h * half, half)]
-            rs.append(send(piece, piece, r_send.at[h], r_recv.at[h], dp, along_y(step)))
+            rs.append(send(piece, piece, r_send.at[0], r_recv.at[h], dp, along_y(step)))
             rs[-1].start()
 
     def filter_step(k, carry):
@@ -343,23 +356,9 @@
         filt_s[k, :, 128:256] = im
         return carry
 
-    lax.fori_loop(0, 33, filter_step, 0)
-
-    relays = []
-
-    def relay(slot, index):
-        piece = up_all.at[slot]
-        relays.append(send(piece, piece, p_send.at[index], p_recv.at[index], dp, partner))
-        relays[-1].start()
-
-    for i, step in enumerate(steps):
-        for h in range(2):
-            if not (NY == 4 and (step, h) in ((1, 0), (-1, 1))):
-                us[step, h].wait_recv()
-        relay(slot_of(-step, 0), 1 + i)
-
-    for copy in ms:
-        copy.wait_recv()
+    lax.fori_loop(0, 33, filter_step, 0, unroll=UNROLL)
+
+    drain(mix_all.at[pl.ds(0, nctx - 1)], m_recv.at[0])
     sections(mix_all)
 
     def conv_step(k, carry):
@@ -371,7 +370,7 @@
         iq[k, 0:CH] = jnp.dot(both, it[k], preferred_element_type=F32)
         return carry
 
-    lax.fori_loop(0, 33, conv_step, 0)
+    lax.fori_loop(0, 33, conv_step, 0, unroll=UNROLL)
     rejoin(0, conv_own)
     cs = []
     for s in range(1, NZH):
@@ -379,59 +378,90 @@
         cs.append(
             send(
                 conv_own.at[pl.ds(to * nnear, nnear)], conv_all.at[zh],
-                c_send.at[s], c_recv.at[s], dp, to * nnear + near,
+                c_send.at[0], c_recv.at[0], dp, to * nnear + near,
             )
         )
         cs[-1].start()
     for i in range(nnear):
         conv_all[zh, i] = conv_own[zh * nnear + i]
 
+    vs = []
+    for s, copy in enumerate(ws, 1):
+        copy.wait_recv()
+        shard = lax.rem(zh + NZH - s, NZH)
+        for t in range(1, NX):
+            there = zl * NX + lax.rem(x + t, NX)
+            piece = w_all.at[shard, mine]
+            vs.append(send(piece, piece, v_send.at[0], v_recv.at[0], there, ctx))
+            vs[-1].start()
+    relays = []
+
+    def relay(slot, index):
+        piece = up_all.at[slot]
+        relays.append(send(piece, piece, p_send.at[0], p_recv.at[index], dp, partner))
+        relays[-1].start()
+
+    for i, step in enumerate(steps):
+        for h in range(2):
+            if not (NY == 4 and (step, h) in ((1, 0), (-1, 1))):
+                us[step, h].wait_recv()
+        relay(slot_of(-step, 0), 1 + i)
+
     far = slot_of(2, 0)
+    loads[4].wait()
+    loads[5].wait()
+    if vs:
+        drain(w_all.at[pl.ds(0, NZH - 1), pl.ds(0, CH - rows)], v_recv.at[0])
+    ss = [[], []]
+
+    def work(yy, k):
+        w = w_all[...].reshape(NZH * CH, depth)
+        up = up_all[pl.ds(yy * NC, NC)].reshape(NC * TOK, depth)
+        both = lax.dot_general(
+            w, up, (((1,), (1,)), ((), ())), preferred_element_type=F32
+        ).astype(BF)
+        for c in range(NC):
+            slot = yy * NC + c
+            gg = both[:, c * TOK : (c + 1) * TOK].reshape(NZH, CH, TOK)
+            gg_all[slot] = gg
+            sc_all[slot] = (gg.astype(F32) * q_all[slot].astype(F32)).astype(BF)
+            n = zh * nnear + slot
+            for s in range(1, NZH):
+                to = lax.rem(zh + s, NZH)
+                for g in range(2):
+                    group = pl.ds(g * HALF, HALF)
+                    ss[g].append(
+                        send(
+                            sc_all.at[slot, to, group], scl_all.at[n, group],
+                            s_send.at[g], s_recv.at[g], dp, to * nnear + near,
+                        )
+                    )
+                ss[0][-1].start()
+            scl_all[n] = sc_all[slot, zh]
+
+    def need(dy):
+        for dc in range(NC):
+            if dy or dc:
+                qs[dy, dc].wait_recv()
+
+    need(0)
+    pair.wait_recv()
+    work(y, 0)
+    for i, step in enumerate(steps):
+        need(step % NY)
+        relays[i].wait_recv()
+        work(lax.rem(y - step + NY, NY), 1 + i)
     if NY == 4:
+        need(2)
         for copy in rs:
             copy.wait_recv()
         relay(far, 3)
-    loads[4].wait()
-    loads[5].wait()
-    for copy in vs + qs:
-        copy.wait_recv()
-    ss = []
-
-    def work(slot, k):
-        w = w_all[...].reshape(NZH * CH, depth)
-        gg = lax.dot_general(
-            w, up_all[slot], (((1,), (1,)), ((), ())), preferred_element_type=F32
-        ).astype(BF)
-        gg = gg.reshape(NZH, CH, TOK)
-        gg_all[slot] = gg
-        sc_all[slot] = (gg.astype(F32) * q_all[slot].astype(F32)).astype(BF)
-        n = zh * nnear + slot
-        for s in range(1, NZH):
-            to = lax.rem(zh + s, NZH)
-            ss.append(
-                send(
-                    sc_all.at[slot, to], scl_all.at[n],
-                    s_send.at[k, s], s_recv.at[k, s], dp, to * nnear + near,
-                )
-            )
-            ss[-1].start()
-        scl_all[n] = sc_all[slot, zh]
-
-    work(near, 0)
-    for i, step in enumerate(steps):
-        work(slot_of(-step, 0), 1 + i)
-    pair.wait_recv()
-    work(slot_of(0, 1), NY)
-    for i, step in enumerate(steps):
-        relays[i].wait_recv()
-        work(slot_of(-step, 1), NY + 1 + i)
-    if NY == 4:
-        work(far, 3)
         relays[2].wait_recv()
-        work(slot_of(2, 1), 7)
-
-    for copy in cs:
-        copy.wait_recv()
+        work(lax.rem(y + 2, NY), 3)
+    for copy in ss[1]:
+        copy.start()
+
+    drain(conv_all.at[pl.ds(0, NZH - 1)], c_recv.at[0])
     for i in range(nnear):
         for h in range(NZH):
             conv = conv_all[h, i].astype(F32)
@@ -447,7 +477,7 @@
         gw_part[to] = jnp.dot(gate[...], up, preferred_element_type=F32).astype(BF)
         if s:
             wxs.append(
-                send(gw_part.at[to], gw_x.at[x], wx_send.at[s], wx_recv.at[s], zl * NX + to, ctx)
+                send(gw_part.at[to], gw_x.at[x], wx_send.at[0], wx_recv.at[0], zl * NX + to, ctx)
             )
             wxs[-1].start()
     gw_x[x] = gw_part[x]
@@ -455,50 +485,63 @@
     for s in range(1, nnear):
         to = lax.rem(near + s, nnear)
         gs.append(
-            send(gq_all.at[to], gq_out.at[:, near], g_send.at[s], g_recv.at[s], dp, zh * nnear + to)
+            send(gq_all.at[to], gq_in.at[:, near], g_send.at[0], g_recv.at[0], dp, zh * nnear + to)
         )
         gs[-1].start()
-    own_g = pltpu.make_async_copy(gq_all.at[near], gq_out.at[:, near], local.at[7])
-    own_g.start()
-
-    for copy in ss:
-        copy.wait_recv()
-    sections(scl_all)
-
-    def back_step(k, carry):
-        gr, gi = forward(k)
-        fr, fi = filt_s[k, :, 0:128], filt_s[k, :, 128:256]
-        mr, mi = mix_s[k, :, 0:128], mix_s[k, :, 128:256]
-        upper = jnp.concatenate([fr * gr + fi * gi, fr * gi - fi * gr], axis=1).astype(BF)
-        lower = jnp.concatenate([mr * gr + mi * gi, mr * gi - mi * gr], axis=1).astype(BF)
-        both = jnp.concatenate([upper, lower], axis=0)
-        iq[k] = jnp.dot(both, it[k], preferred_element_type=F32)
-        return carry
-
-    lax.fori_loop(0, 33, back_step, 0)
-    rejoin(0, back_own)
-    bs = []
-    for s in range(1, nctx):
-        to = lax.rem(ctx + s, nctx)
-        bs.append(send(back_own.at[to], back_out.at[ctx], b_send.at[s], b_recv.at[s], dp, to))
-        bs[-1].start()
-    own_b = pltpu.make_async_copy(back_own.at[ctx], back_out.at[ctx], local.at[8])
-    own_b.start()
-    rejoin(CH, fg_own)
-    fxs = []
-    for s in range(1, NX):
-        to = lax.rem(x + s, NX)
-        fxs.append(
-            send(
-                fg_own.at[pl.ds(pl.multiple_of(to * rows, rows), rows)], fg_x.at[x],
-                fx_send.at[s], fx_recv.at[s], zl * NX + to, ctx,
+    for h in range(NZH):
+        gq_in[h, near] = gq_all[near, h]
+
+    bs, fxs = [[], []], []
+    lanes = seq // NX
+
+    def back_group(g):
+        group = slice(g * HALF, (g + 1) * HALF)
+        group_ds = pl.ds(g * HALF, HALF)
+
+        def back_step(k, carry):
+            full = jnp.dot(part[k, group].astype(BF), ft[k], preferred_element_type=F32)
+            gr, gi = full[:, 0:128], full[:, 128:256]
+            fr, fi = filt_s[k, group, 0:128], filt_s[k, group, 128:256]
+            mr, mi = mix_s[k, group, 0:128], mix_s[k, group, 128:256]
+            upper = jnp.concatenate([fr * gr + fi * gi, fr * gi - fi * gr], axis=1).astype(BF)
+            lower = jnp.concatenate([mr * gr + mi * gi, mr * gi - mi * gr], axis=1).astype(BF)
+            both = jnp.concatenate([upper, lower], axis=0)
+            out = jnp.dot(both, it[k], preferred_element_type=F32)
+            iq[k, group] = out[0:HALF]
+            iq[k, CH + g * HALF : CH + (g + 1) * HALF] = out[HALF:CH]
+            return carry
+
+        drain(scl_all.at[pl.ds(0, (NZH - 1) * nnear), group_ds], s_recv.at[g])
+        sections(scl_all, g * HALF // 16, HALF // 16)
+        lax.fori_loop(0, 33, back_step, 0, unroll=UNROLL)
+        rejoin(0, back_own, g * HALF // 16, HALF // 16)
+        for s, to in enumerate(ctx_order(), 1):
+            bs[g].append(
+                send(
+                    back_own.at[to, group], back_in.at[ctx, group],
+                    b_send.at[0], b_recv.at[0], dp, to,
+                )
             )
-        )
-        fxs[-1].start()
-    fg_x[x] = fg_own[mine]
-
-    for copy in wxs:
-        copy.wait_recv()
+            if g == 0:
+                bs[g][-1].start()
+        rejoin(CH, fg_own, g * HALF // 16, HALF // 16)
+        for s in range(1, NX):
+            to = lax.rem(x + s, NX)
+            fxs.append(
+                send(
+                    fg_own.at[group, pl.ds(pl.multiple_of(to * lanes, lanes), lanes)],
+                    fg_x.at[x, group],
+                    fx_send.at[0], fx_recv.at[0], zl * NX + to, ctx,
+                )
+            )
+            fxs[-1].start()
+
+    back_group(0)
+    back_group(1)
+    back_in[ctx] = back_own[ctx]
+    fg_x[x] = fg_own[:, pl.ds(pl.multiple_of(x * lanes, lanes), lanes)]
+    if NX > 1:
+        drain(gw_x.at[pl.ds(0, NX - 1)], wx_recv.at[0])
     for h in range(NZH):
         total = gw_x[0, h * CH : (h + 1) * CH].astype(F32)
         for i in range(1, NX):
@@ -514,42 +557,26 @@
                 zs.append(
                     send(
                         gw_mid.at[to, tl], gw_z.at[zh * NZL + zl],
-                        wz_send.at[k], wz_recv.at[k], tl * NX + x, to * nnear + near,
+                        wz_send.at[0], wz_recv.at[0], tl * NX + x, to * nnear + near,
                     )
                 )
                 zs[-1].start()
     gw_z[zh * NZL + zl] = gw_mid[zh, zl]
 
-    for copy in fxs:
-        copy.wait_recv()
+    if NX > 1:
+        drain(fg_x.at[pl.ds(0, NX - 1)], fx_recv.at[0])
     total = fg_x[0].astype(F32)
     for i in range(1, NX):
         total = total + fg_x[i].astype(F32)
-    for i in range(NZL):
-        fg_half[i] = total[:, i * span : (i + 1) * span].astype(BF)
+    fg_half[...] = total.astype(BF)
     fzs = []
     for s in range(1, NZL):
         to = lax.rem(zl + s, NZL)
-        fzs.append(
-            send(fg_half.at[to], fg_z.at[zl], fz_send.at[s], fz_recv.at[s], to * NX + x, ctx)
-        )
+        fzs.append(send(fg_half, fg_z.at[zl], fz_send.at[s], fz_recv.at[s], to * NX + x, ctx))
         fzs[-1].start()
-    fg_z[zl] = fg_half[zl]
-
-    for copy in zs:
-        copy.wait_recv()
-    total = gw_z[0].astype(F32)
-    for i in range(1, nz):
-        total = total + gw_z[i].astype(F32)
-    gw_fin[...] = total.astype(BF)
-    was = []
-    wslot = gw_out.at[:, pl.ds(pl.multiple_of((x * NZL + zl) * narrow, narrow), narrow)]
-    for s in range(1, ndp):
-        to = lax.rem(dp + s, ndp)
-        was.append(send(gw_fin, wslot, wa_send.at[s], wa_recv.at[s], to, ctx))
-        was[-1].start()
-    own_wa = pltpu.make_async_copy(gw_fin, wslot, local.at[9])
-    own_wa.start()
+    fg_z[zl] = fg_half[...]
+    for copy in bs[1]:
+        copy.start()
 
     for copy in fzs:
         copy.wait_recv()
@@ -558,21 +585,93 @@
         total = total + fg_z[i].astype(F32)
     fg_fin[...] = total.astype(BF)
     fas = []
-    fslot = fg_out.at[mine, pl.ds(pl.multiple_of(zl * span, span), span)]
-    for s in range(1, ndp):
-        to = lax.rem(dp + s, ndp)
-        fas.append(send(fg_fin, fslot, fa_send.at[s], fa_recv.at[s], to, ctx))
+    fslot = fg_out.at[:, pl.ds(pl.multiple_of(x * lanes, lanes), lanes)]
+    for s in range(1, NX):
+        to = zl * NX + lax.rem(x + s, NX)
+        fas.append(send(fg_fin, fslot, fa_send.at[0], fa_recv.at[0], to, ctx))
         fas[-1].start()
-    own_fa = pltpu.make_async_copy(fg_fin, fslot, local.at[10])
+    own_fa = pltpu.make_async_copy(fg_fin, fslot, local.at[11])
     own_fa.start()
 
-    for copy in (own_g, own_b, own_wa, own_fa):
+    drain(gw_z.at[pl.ds(0, nz - 1)], wz_recv.at[0])
+    total = gw_z[0].astype(F32)
+    for i in range(1, nz):
+        total = total + gw_z[i].astype(F32)
+    gw_fin[...] = total.astype(BF)
+    gw_sum[zl] = gw_fin[...]
+    was = []
+    if NZL > 1:
+        pair_w = send(gw_fin, gw_sum.at[zl], wz_send.at[1], wz_recv.at[1], other, ctx)
+        pair_w.start()
+
+    def spread(l, k):
+        wslot = gw_out.at[:, pl.ds(pl.multiple_of((x * NZL + l) * narrow, narrow), narrow)]
+        for s in range(1, NX):
+            to = zl * NX + lax.rem(x + s, NX)
+            was.append(send(gw_sum.at[l], wslot, wa_send.at[0], wa_recv.at[0], to, ctx))
+            was[-1].start()
+        own = pltpu.make_async_copy(gw_sum.at[l], wslot, local.at[9 + k])
+        own.start()
+        return own
+
+    own_wa = [spread(zl, 0)]
+    drain(gq_in.at[:, pl.ds(0, nnear - 1)], g_recv.at[0])
+
+    def query_rows(j, carry):
+        cols = pl.ds(pl.multiple_of(j * 2 * CH, 2 * CH), 2 * CH)
+        first = 2 * j
+        h, i = first // nnear, lax.rem(first, nnear)
+        block = jnp.concatenate([gq_in[h, i], gq_in[h, i + 1]], axis=0)
+        q_own[:, cols] = block.astype(F32).T.astype(BF)
+        return carry
+
+    lax.fori_loop(0, nctx // 2, query_rows, 0)
+    out_q = pltpu.make_async_copy(q_own, gq_out, local.at[7])
+    out_q.start()
+    if NZL > 1:
+        pair_w.wait_recv()
+        own_wa.append(spread(lax.rem(zl + 1, NZL), 1))
+    drain(back_in.at[pl.ds(0, nctx - 1)], b_recv.at[0])
+
+    def back_rows(j, carry):
+        cols = pl.ds(pl.multiple_of(j * 2 * CH, 2 * CH), 2 * CH)
+        block = jnp.concatenate([back_in[2 * j], back_in[2 * j + 1]], axis=0)
+        k_own[:, cols] = block.astype(F32).T.astype(BF)
+        return carry
+
+    lax.fori_loop(0, nctx // 2, back_rows, 0)
+    out_b = pltpu.make_async_copy(k_own, back_out, local.at[8])
+    out_b.start()
+    for copy in [out_q, out_b, own_fa] + own_wa:
         copy.wait()
-    sent = ms + ws + list(us.values()) + [pair] + qs + vs + rs + relays + cs + ss
-    for copy in sent + wxs + fxs + fzs + zs:
-        copy.wait_send()
-    for copy in gs + bs + was + fas:
-        copy.wait()
+    if NZL > 1:
+        pair_w.wait_send()
+        for copy in fzs:
+            copy.wait_send()
+    drain(mix_all.at[pl.ds(0, nctx - 1)], m_send.at[0])
+    drain(up_all.at[pl.ds(0, 1 + len(steps) + (NY == 4))], p_send.at[0])
+    if steps:
+        drain(up_all.at[pl.ds(0, len(steps))], u_send.at[0])
+    if NY == 4:
+        drain(up_all.at[0], r_send.at[0])
+    drain(q_all.at[pl.ds(0, nnear - 1)], q_send.at[0])
+    drain(w_all.at[pl.ds(0, NZH - 1), pl.ds(0, rows)], w_send.at[0])
+    if vs:
+        drain(w_all.at[pl.ds(0, NZH - 1), pl.ds(0, CH - rows)], v_send.at[0])
+    for g in range(2):
+        drain(scl_all.at[pl.ds(0, (NZH - 1) * nnear), pl.ds(0, HALF)], s_send.at[g])
+    drain(conv_all.at[pl.ds(0, NZH - 1)], c_send.at[0])
+    drain(back_in.at[pl.ds(0, nctx - 1)], b_send.at[0])
+    drain(gq_in.at[:, pl.ds(0, nnear - 1)], g_send.at[0])
+    drain(gw_z.at[pl.ds(0, nz - 1)], wz_send.at[0])
+    if NX > 1:
+        drain(fg_x.at[pl.ds(0, NX - 1)], fx_send.at[0])
+        drain(gw_x.at[pl.ds(0, NX - 1)], wx_send.at[0])
+        drain(fg_x.at[pl.ds(0, NX - 1)], fa_send.at[0])
+        gw_bytes = gw_x.at[pl.ds(0, NX - 1), pl.ds(0, CH), pl.ds(0, NZL * narrow)]
+        drain(gw_bytes, wa_send.at[0])
+        drain(gw_bytes, wa_recv.at[0])
+        drain(fg_x.at[pl.ds(0, NX - 1)], fa_recv.at[0])
 
 
 def mixer_call(keys, values, queries, up, filters, w):
@@ -580,7 +679,7 @@
     depth = up.shape[-1]
     seq = nctx * TOK
     wide, narrow = depth // NX, depth // NX // NZL
-    rows, span = CH // NX, seq // NZL
+    rows = CH // NX
     i = np.arange(128)
     angle = 2.0 * np.pi * ((i[:, None] * i[None, :]) % 128) / 128
     step = np.broadcast_to((2.0 * np.pi * i / 8192)[:, None], (128, 128))
@@ -592,16 +691,16 @@
     near4 = (nnear, NZH, CH, TOK)
     chans = (nctx, CH, TOK)
     spec = (33, CH, 256)
-    pairs = [
-        (nctx,), (4,), (2,), (4,), (nnear,), (NZH,), (NZH, NX), (nnear, NZH), (NZH,), (nctx,),
-        (NX,), (NZL,), (ndp,), (nnear,), (NX,), (nz,), (ndp,),
+    sems = [
+        1, 1, 1, 4, 1, 2, 1, 4, 1, nnear, 1, NZH, 1, 1, 2, 2, 1, 1, 1, 1,
+        1, 1, NZL, NZL, 1, 1, 1, 1, 1, 1, 2, 2, 1, 1,
     ]
     return pl.pallas_call(
         mixer_kernel,
         name="mixer",
         out_shape=[
-            jax.ShapeDtypeStruct((NZH, nnear, CH, TOK), BF),
-            jax.ShapeDtypeStruct(chans, BF),
+            jax.ShapeDtypeStruct((TOK, nctx * CH), BF),
+            jax.ShapeDtypeStruct((TOK, nctx * CH), BF),
             jax.ShapeDtypeStruct((CH, seq), BF),
             jax.ShapeDtypeStruct((CH, depth), BF),
         ],
@@ -634,17 +733,20 @@
             pltpu.VMEM((CH, seq), BF),
             pltpu.VMEM((NZH * CH, nnear * TOK), BF),
             pltpu.VMEM(near4, BF),
-            pltpu.VMEM((NX, rows, seq), BF),
-            pltpu.VMEM((NZL, rows, span), BF),
-            pltpu.VMEM((NZL, rows, span), BF),
-            pltpu.VMEM((rows, span), BF),
+            pltpu.VMEM((NZH, nnear, CH, TOK), BF),
+            pltpu.VMEM(chans, BF),
+            pltpu.VMEM((NX, CH, seq // NX), BF),
+            pltpu.VMEM((CH, seq // NX), BF),
+            pltpu.VMEM((NZL, CH, seq // NX), BF),
+            pltpu.VMEM((CH, seq // NX), BF),
             pltpu.VMEM((NX, NZH * CH, wide), BF),
             pltpu.VMEM((NX, NZH * CH, wide), BF),
             pltpu.VMEM((NZH, NZL, CH, narrow), BF),
             pltpu.VMEM((nz, CH, narrow), BF),
             pltpu.VMEM((CH, narrow), BF),
+            pltpu.VMEM((NZL, CH, narrow), BF),
         ]
-        + [dma(n) for n in pairs for _ in range(2)]
+        + [dma((n,)) for n in sems]
         + [dma((12,))],
         compiler_params=pltpu.CompilerParams(
             collective_id=0, has_side_effects=True, vmem_limit_bytes=60 << 20
@@ -653,16 +755,14 @@
 
 
 def per_device(queries, keys, values, upstream, filters, out_weight):
-    nctx = NZH * NY * NC
     key_rows, value_rows = keys[0], values[0]
     gq, back, fg, gw = mixer_call(
         key_rows, value_rows, queries[0], upstream[0], filters, out_weight
     )
-    grad_queries = gq.reshape(nctx * CH, TOK).T
-    back_wide = back.reshape(nctx * CH, TOK).T.astype(F32)
+    back_wide = back.astype(F32)
     grad_keys = (back_wide * value_rows.astype(F32)).astype(BF)
     grad_values = (back_wide * key_rows.astype(F32)).astype(BF)
-    return (grad_queries[None], grad_keys[None], grad_values[None], fg.astype(F32), gw.astype(F32))
+    return (gq[None], grad_keys[None], grad_values[None], fg.astype(F32), gw.astype(F32))
 
 
 def solution(mesh):

time: 124 us -> 92.4 us (0.75)
  Pallas kernels: 116 us -> 86 us
    pallas_call x1, Pallas kernels: 116 us -> 86 us  [mixer_call(): pl.pallas_call(mixer_kernel, name='mixer', out_shape=[jax.ShapeDtypeStruc...]
where the time goes in v1:
time: 92.4 us; the launch traced here: 92.2 us
  Pallas kernels  86 us (93%)
  other arithmetic  4.25 us (5%)
  local copies, waits for them, and re-layouts  1.21 us (1%)
    pallas_call x1, Pallas kernels, mixer_call(): pl.pallas_call(mixer_kernel, name='mixer', out_shape=[jax.ShapeDtypeStruc...  86 us
    broadcast_in_dim x1, other arithmetic, per_device(): grad_values[None]  2.38 us

profile of v1, /device:TPU:1, one launch (start us, length us, event | category | flops | bytes accessed | tf_op | source)
XLA Modules:
  0.0 92.2 jit_solution(3026738433371760798)
XLA Ops:
  0.6 0.0 copy-start
  0.6 0.0 copy-start.1
  0.7 86.0 %mixer.1 = (bf16[128,2048]{1,0:T(8,128)(2,1)}, bf16[128,2048]{1,0:T(8,128)(2,1)}, bf16[64,4096]{1,0:T(8,128)(2,1)}, bf16[64,2048]{1,0:T(8,128)(2,1)}) custom-call(bf16[128,2048]{1,0:T(8,128)(2,1)} %bitcast.11, bf16[128,2048]{1,0:T(8,128)(2,1)} %bitcast.12, bf16[128,2048]{1,0:T(8,128)(2,1)} %bitcast.14, bf16[128,2048]{1,0:T(8,128)(2,1)} %bitcast.15, ...), custom_call_target="tpu_custom_call" | custom-call | tf_op jit(solution)/shard_map/mixer/pallas_call | solution.py:698
  86.7 0.0 copy-done
  86.7 0.0 copy-done.1
  86.7 0.0 copy-start.2
  86.7 2.4 %fusion.2 = (bf16[1,128,2048]{2,1,0:T(8,128)(2,1)}, bf16[1,128,2048]{2,1,0:T(8,128)(2,1)}) fusion(bf16[128,2048]{1,0:T(8,128)(2,1)} %get-tuple-element.10, bf16[1,128,2048]{2,1,0:T(8,128)(2,1)S(1)} %copy-done, bf16[1,128,2048]{2,1,0:T(8,128)(2,1)S(1)} %copy-done.1), kind=kLoop, calls=%fused_computation.4 | loop fusion | flops 1835008 | bytes 2621440 | tf_op jit(solution)/shard_map/broadcast_in_dim | solution.py:765
  89.1 0.0 copy-done.2
  89.1 0.0 copy-start.4
  89.1 1.0 %convert_element_type.26 = f32[64,4096]{1,0:T(8,128)} convert(bf16[64,4096]{1,0:T(8,128)(2,1)S(1)} %copy-done.2) | non-fusion elementwise | flops 262144 | bytes 1572864 | tf_op jit(solution)/shard_map/convert_element_type | solution.py:765
  90.2 0.0 copy-start.3
  90.2 0.0 copy-done.4
  90.2 0.8 convert_element_type.27
  91.0 0.4 copy-done.3
  91.4 0.8 copy.18
Async XLA Ops:
  0.6 86.1 %copy-start = (bf16[1,128,2048]{2,1,0:T(8,128)(2,1)S(1)}, bf16[1,128,2048]{2,1,0:T(8,128)(2,1)}, u32[]{:S(2)}) copy-start(bf16[1,128,2048]{2,1,0:T(8,128)(2,1)} %param.13) | copy-start | bytes 1572868
  0.6 86.1 %copy-start.1 = (bf16[1,128,2048]{2,1,0:T(8,128)(2,1)S(1)}, bf16[1,128,2048]{2,1,0:T(8,128)(2,1)}, u32[]{:S(2)}) copy-start(bf16[1,128,2048]{2,1,0:T(8,128)(2,1)} %param.14) | copy-start | bytes 1572868
  86.7 2.4 %copy-start.2 = (bf16[64,4096]{1,0:T(8,128)(2,1)S(1)}, bf16[64,4096]{1,0:T(8,128)(2,1)}, u32[]{:S(2)}) copy-start(bf16[64,4096]{1,0:T(8,128)(2,1)} %get-tuple-element.11) | copy-start | bytes 1572868
  89.1 1.0 %copy-start.4 = (bf16[64,2048]{1,0:T(8,128)(2,1)S(1)}, bf16[64,2048]{1,0:T(8,128)(2,1)}, u32[]{:S(2)}) copy-start(bf16[64,2048]{1,0:T(8,128)(2,1)} %get-tuple-element.12) | copy-start | bytes 786436
  90.2 1.2 %copy-start.3 = (bf16[128,2048]{1,0:T(8,128)(2,1)S(1)}, bf16[128,2048]{1,0:T(8,128)(2,1)}, u32[]{:S(2)}) copy-start(bf16[128,2048]{1,0:T(8,128)(2,1)} %get-tuple-element.9) | copy-start | bytes 1572868

commit v2 on v1

--- a/solution.py
+++ b/solution.py
@@ -13,6 +13,7 @@
 TOK, CH = 128, 64
 HALF = CH // 2
 UNROLL = 11
+FINISH_STEPS = 2
 BF, F32 = jnp.bfloat16, jnp.float32
 MESH = pl.DeviceIdType.MESH
 
@@ -151,10 +152,10 @@
 
 def mixer_kernel(
     key_ref, value_ref, query_ref, up_ref, filt_ref, w_ref,
-    cos_ref, sin_ref, wc_ref, ws_ref, wct_ref, wst_ref,
+    table_ref,
     gq_out, back_out, fg_out, gw_out,
     k_own, v_own, q_own, f_own, mix_t, q_t, mix_all, q_all, up_all, w_all, gg_all, sc_all, scl_all,
-    ft, it, tab, part, filt_s, mix_s, iq, conv_own, conv_all, back_own, fg_own, gate, gq_all, gq_in, back_in,
+    ft, it, tab, wave, part, filt_s, mix_s, iq, conv_own, conv_all, back_own, fg_own, gate, gq_all, gq_in, back_in,
     fg_x, fg_half, fg_z, fg_fin, gw_part, gw_x, gw_mid, gw_z, gw_fin, gw_sum,
     m_send, m_recv, u_send, u_recv, r_send, r_recv, p_send, p_recv, q_send, q_recv,
     w_send, w_recv, v_send, v_recv, s_send, s_recv, c_send, c_recv, b_send, b_recv,
@@ -171,8 +172,9 @@
     wide, narrow = depth // NX, depth // NX // NZL
     half = TOK // 2
 
+    turns = sorted(range(NZH), key=lambda a: -min(a, NZH - a))
+
     def ctx_order():
-        turns = sorted(range(NZH), key=lambda a: -min(a, NZH - a))
         return [
             lax.rem(zh + a, NZH) * nnear + lax.rem(near + b, nnear)
             for a in turns
@@ -198,6 +200,7 @@
         pltpu.make_async_copy(filt_ref, f_own, local.at[3]),
         pltpu.make_async_copy(up_ref, up_all.at[near], local.at[4]),
         pltpu.make_async_copy(w_ref, w_all.at[zh], local.at[5]),
+        pltpu.make_async_copy(table_ref, wave, local.at[6]),
     ]
     for copy in loads:
         copy.start()
@@ -216,17 +219,21 @@
     mix_all[ctx] = mix_t[ctx]
     pl.semaphore_wait(barrier, len(peers))
 
-    ms = []
-    for s, to in enumerate(ctx_order(), 1):
-        ms.append(send(mix_t.at[to], mix_all.at[ctx], m_send.at[0], m_recv.at[0], dp, to))
-        ms[-1].start()
-
+    def send_mixed(g):
+        group = pl.ds(g * HALF, HALF)
+        for to in ctx_order():
+            send(
+                mix_t.at[to, group], mix_all.at[ctx, group], m_send.at[g], m_recv.at[g], dp, to
+            ).start()
+
+    send_mixed(0)
     mine = pl.ds(pl.multiple_of(x * rows, rows), rows)
     ws = []
     for s in range(1, NZH):
         there = lax.rem(zh + s, NZH) * nnear + near
         ws.append(send(w_ref.at[mine], w_all.at[zh, mine], w_send.at[0], w_recv.at[s], dp, there))
         ws[-1].start()
+    send_mixed(1)
 
     def along_y(step):
         return zh * nnear + lax.rem(y + step + NY, NY) * NC + core
@@ -273,10 +280,11 @@
     q_all[near] = q_t[near]
 
     scale = 2.0 / 8192
-    tab[0] = cos_ref[...]
-    tab[1] = -sin_ref[...]
-    tab[2] = cos_ref[...] * scale
-    tab[3] = sin_ref[...] * scale
+    loads[6].wait()
+    tab[0] = wave[0]
+    tab[1] = -wave[1]
+    tab[2] = wave[0] * scale
+    tab[3] = wave[1] * scale
 
     def build(k, carry):
         a, b = tab[0], tab[1]
@@ -284,7 +292,7 @@
         ft[k, 128:256, 128:256] = a.astype(BF)
         ft[k, 0:128, 128:256] = b.astype(BF)
         ft[k, 128:256, 0:128] = (-b).astype(BF)
-        c, s = wc_ref[...], ws_ref[...]
+        c, s = wave[2], wave[3]
         tab[0] = a * c + b * s
         tab[1] = b * c - a * s
         a, b = tab[2], tab[3]
@@ -292,7 +300,7 @@
         it[k, 128:256, 128:256] = a.astype(BF)
         it[k, 0:128, 128:256] = b.astype(BF)
         it[k, 128:256, 0:128] = (-b).astype(BF)
-        c, s = wct_ref[...], wst_ref[...]
+        c, s = wave[4], wave[5]
         tab[2] = a * c - b * s
         tab[3] = b * c + a * s
         return carry
@@ -342,6 +350,14 @@
     loads[3].wait()
     sections(None)
 
+    def filter_step(k, carry):
+        re, im = forward(k)
+        filt_s[k, :, 0:128] = re
+        filt_s[k, :, 128:256] = im
+        return carry
+
+    lax.fori_loop(0, 33, filter_step, 0, unroll=UNROLL)
+
     rs = []
     if NY == 4:
         for step, h in ((1, 0), (-1, 1)):
@@ -350,41 +366,32 @@
             rs.append(send(piece, piece, r_send.at[0], r_recv.at[h], dp, along_y(step)))
             rs[-1].start()
 
-    def filter_step(k, carry):
-        re, im = forward(k)
-        filt_s[k, :, 0:128] = re
-        filt_s[k, :, 128:256] = im
-        return carry
-
-    lax.fori_loop(0, 33, filter_step, 0, unroll=UNROLL)
-
-    drain(mix_all.at[pl.ds(0, nctx - 1)], m_recv.at[0])
-    sections(mix_all)
-
-    def conv_step(k, carry):
-        mr, mi = forward(k)
-        mix_s[k, :, 0:128] = mr
-        mix_s[k, :, 128:256] = mi
-        fr, fi = filt_s[k, :, 0:128], filt_s[k, :, 128:256]
-        both = jnp.concatenate([fr * mr - fi * mi, fr * mi + fi * mr], axis=1).astype(BF)
-        iq[k, 0:CH] = jnp.dot(both, it[k], preferred_element_type=F32)
-        return carry
-
-    lax.fori_loop(0, 33, conv_step, 0, unroll=UNROLL)
-    rejoin(0, conv_own)
-    cs = []
-    for s in range(1, NZH):
-        to = lax.rem(zh + s, NZH)
-        cs.append(
+    def conv_group(g):
+        group = slice(g * HALF, (g + 1) * HALF)
+        group_ds = pl.ds(g * HALF, HALF)
+
+        def conv_step(k, carry):
+            full = jnp.dot(part[k, group].astype(BF), ft[k], preferred_element_type=F32)
+            mr, mi = full[:, 0:128], full[:, 128:256]
+            mix_s[k, group, 0:128] = mr
+            mix_s[k, group, 128:256] = mi
+            fr, fi = filt_s[k, group, 0:128], filt_s[k, group, 128:256]
+            both = jnp.concatenate([fr * mr - fi * mi, fr * mi + fi * mr], axis=1).astype(BF)
+            iq[k, group] = jnp.dot(both, it[k], preferred_element_type=F32)
+            return carry
+
+        drain(mix_all.at[pl.ds(0, nctx - 1), group_ds], m_recv.at[g])
+        sections(mix_all, g * HALF // 16, HALF // 16)
+        lax.fori_loop(0, 33, conv_step, 0, unroll=UNROLL)
+        rejoin(0, conv_own, g * HALF // 16, HALF // 16)
+        for s in turns[:-1]:
+            to = lax.rem(zh + s, NZH)
             send(
-                conv_own.at[pl.ds(to * nnear, nnear)], conv_all.at[zh],
+                conv_own.at[pl.ds(to * nnear, nnear), group_ds], conv_all.at[zh, :, group_ds],
                 c_send.at[0], c_recv.at[0], dp, to * nnear + near,
-            )
-        )
-        cs[-1].start()
-    for i in range(nnear):
-        conv_all[zh, i] = conv_own[zh * nnear + i]
-
+            ).start()
+
+    conv_group(0)
     vs = []
     for s, copy in enumerate(ws, 1):
         copy.wait_recv()
@@ -394,6 +401,10 @@
             piece = w_all.at[shard, mine]
             vs.append(send(piece, piece, v_send.at[0], v_recv.at[0], there, ctx))
             vs[-1].start()
+    conv_group(1)
+    for i in range(nnear):
+        conv_all[zh, i] = conv_own[zh * nnear + i]
+
     relays = []
 
     def relay(slot, index):
@@ -406,7 +417,6 @@
             if not (NY == 4 and (step, h) in ((1, 0), (-1, 1))):
                 us[step, h].wait_recv()
         relay(slot_of(-step, 0), 1 + i)
-
     far = slot_of(2, 0)
     loads[4].wait()
     loads[5].wait()
@@ -426,7 +436,7 @@
             gg_all[slot] = gg
             sc_all[slot] = (gg.astype(F32) * q_all[slot].astype(F32)).astype(BF)
             n = zh * nnear + slot
-            for s in range(1, NZH):
+            for s in turns[:-1]:
                 to = lax.rem(zh + s, NZH)
                 for g in range(2):
                     group = pl.ds(g * HALF, HALF)
@@ -436,7 +446,6 @@
                             s_send.at[g], s_recv.at[g], dp, to * nnear + near,
                         )
                     )
-                ss[0][-1].start()
             scl_all[n] = sc_all[slot, zh]
 
     def need(dy):
@@ -451,6 +460,10 @@
         need(step % NY)
         relays[i].wait_recv()
         work(lax.rem(y - step + NY, NY), 1 + i)
+    drain(conv_all.at[pl.ds(0, NZH - 1)], c_send.at[0])
+    for copy in ss[0]:
+        copy.start()
+    started = len(ss[0])
     if NY == 4:
         need(2)
         for copy in rs:
@@ -458,7 +471,7 @@
         relay(far, 3)
         relays[2].wait_recv()
         work(lax.rem(y + 2, NY), 3)
-    for copy in ss[1]:
+    for copy in ss[0][started:] + ss[1]:
         copy.start()
 
     drain(conv_all.at[pl.ds(0, NZH - 1)], c_recv.at[0])
@@ -514,16 +527,6 @@
         drain(scl_all.at[pl.ds(0, (NZH - 1) * nnear), group_ds], s_recv.at[g])
         sections(scl_all, g * HALF // 16, HALF // 16)
         lax.fori_loop(0, 33, back_step, 0, unroll=UNROLL)
-        rejoin(0, back_own, g * HALF // 16, HALF // 16)
-        for s, to in enumerate(ctx_order(), 1):
-            bs[g].append(
-                send(
-                    back_own.at[to, group], back_in.at[ctx, group],
-                    b_send.at[0], b_recv.at[0], dp, to,
-                )
-            )
-            if g == 0:
-                bs[g][-1].start()
         rejoin(CH, fg_own, g * HALF // 16, HALF // 16)
         for s in range(1, NX):
             to = lax.rem(x + s, NX)
@@ -535,6 +538,16 @@
                 )
             )
             fxs[-1].start()
+        rejoin(0, back_own, g * HALF // 16, HALF // 16)
+        for s, to in enumerate(ctx_order(), 1):
+            bs[g].append(
+                send(
+                    back_own.at[to, group], back_in.at[ctx, group],
+                    b_send.at[0], b_recv.at[0], dp, to,
+                )
+            )
+            if g == 0:
+                bs[g][-1].start()
 
     back_group(0)
     back_group(1)
@@ -575,9 +588,30 @@
         fzs.append(send(fg_half, fg_z.at[zl], fz_send.at[s], fz_recv.at[s], to * NX + x, ctx))
         fzs[-1].start()
     fg_z[zl] = fg_half[...]
+    drain(gw_z.at[pl.ds(0, nz - 1)], wz_recv.at[0])
+    total = gw_z[0].astype(F32)
+    for i in range(1, nz):
+        total = total + gw_z[i].astype(F32)
+    gw_fin[...] = total.astype(BF)
+    gw_sum[zl] = gw_fin[...]
+    was = []
+    if NZL > 1:
+        pair_w = send(gw_fin, gw_sum.at[zl], wz_send.at[1], wz_recv.at[1], other, ctx)
+        pair_w.start()
+
+    def spread(l, k):
+        wslot = gw_out.at[:, pl.ds(pl.multiple_of((x * NZL + l) * narrow, narrow), narrow)]
+        for s in range(1, NX):
+            to = zl * NX + lax.rem(x + s, NX)
+            was.append(send(gw_sum.at[l], wslot, wa_send.at[0], wa_recv.at[0], to, ctx))
+            was[-1].start()
+        own = pltpu.make_async_copy(gw_sum.at[l], wslot, local.at[9 + k])
+        own.start()
+        return own
+
     for copy in bs[1]:
         copy.start()
-
+    own_wa = [spread(zl, 0)]
     for copy in fzs:
         copy.wait_recv()
     total = fg_z[0].astype(F32)
@@ -593,28 +627,6 @@
     own_fa = pltpu.make_async_copy(fg_fin, fslot, local.at[11])
     own_fa.start()
 
-    drain(gw_z.at[pl.ds(0, nz - 1)], wz_recv.at[0])
-    total = gw_z[0].astype(F32)
-    for i in range(1, nz):
-        total = total + gw_z[i].astype(F32)
-    gw_fin[...] = total.astype(BF)
-    gw_sum[zl] = gw_fin[...]
-    was = []
-    if NZL > 1:
-        pair_w = send(gw_fin, gw_sum.at[zl], wz_send.at[1], wz_recv.at[1], other, ctx)
-        pair_w.start()
-
-    def spread(l, k):
-        wslot = gw_out.at[:, pl.ds(pl.multiple_of((x * NZL + l) * narrow, narrow), narrow)]
-        for s in range(1, NX):
-            to = zl * NX + lax.rem(x + s, NX)
-            was.append(send(gw_sum.at[l], wslot, wa_send.at[0], wa_recv.at[0], to, ctx))
-            was[-1].start()
-        own = pltpu.make_async_copy(gw_sum.at[l], wslot, local.at[9 + k])
-        own.start()
-        return own
-
-    own_wa = [spread(zl, 0)]
     drain(gq_in.at[:, pl.ds(0, nnear - 1)], g_recv.at[0])
 
     def query_rows(j, carry):
@@ -648,7 +660,8 @@
         pair_w.wait_send()
         for copy in fzs:
             copy.wait_send()
-    drain(mix_all.at[pl.ds(0, nctx - 1)], m_send.at[0])
+    for g in range(2):
+        drain(mix_all.at[pl.ds(0, nctx - 1), pl.ds(0, HALF)], m_send.at[g])
     drain(up_all.at[pl.ds(0, 1 + len(steps) + (NY == 4))], p_send.at[0])
     if steps:
         drain(up_all.at[pl.ds(0, len(steps))], u_send.at[0])
@@ -660,7 +673,6 @@
         drain(w_all.at[pl.ds(0, NZH - 1), pl.ds(0, CH - rows)], v_send.at[0])
     for g in range(2):
         drain(scl_all.at[pl.ds(0, (NZH - 1) * nnear), pl.ds(0, HALF)], s_send.at[g])
-    drain(conv_all.at[pl.ds(0, NZH - 1)], c_send.at[0])
     drain(back_in.at[pl.ds(0, nctx - 1)], b_send.at[0])
     drain(gq_in.at[:, pl.ds(0, nnear - 1)], g_send.at[0])
     drain(gw_z.at[pl.ds(0, nz - 1)], wz_send.at[0])
@@ -684,15 +696,14 @@
     angle = 2.0 * np.pi * ((i[:, None] * i[None, :]) % 128) / 128
     step = np.broadcast_to((2.0 * np.pi * i / 8192)[:, None], (128, 128))
     tables = [np.cos(angle), np.sin(angle), np.cos(step), np.sin(step), np.cos(step.T), np.sin(step.T)]
-    tables = [jnp.asarray(np.ascontiguousarray(t), F32) for t in tables]
+    tables = jnp.asarray(np.stack(tables), F32)
     dma = pltpu.SemaphoreType.DMA
     hbm = pl.BlockSpec(memory_space=pl.ANY)
-    vmem = pl.BlockSpec(memory_space=pltpu.VMEM)
     near4 = (nnear, NZH, CH, TOK)
     chans = (nctx, CH, TOK)
     spec = (33, CH, 256)
     sems = [
-        1, 1, 1, 4, 1, 2, 1, 4, 1, nnear, 1, NZH, 1, 1, 2, 2, 1, 1, 1, 1,
+        2, 2, 1, 4, 1, 2, 1, 4, 1, nnear, 1, NZH, 1, 1, 2, 2, 1, 1, 1, 1,
         1, 1, NZL, NZL, 1, 1, 1, 1, 1, 1, 2, 2, 1, 1,
     ]
     return pl.pallas_call(
@@ -704,7 +715,7 @@
             jax.ShapeDtypeStruct((CH, seq), BF),
             jax.ShapeDtypeStruct((CH, depth), BF),
         ],
-        in_specs=[hbm] * 6 + [vmem] * 6,
+        in_specs=[hbm] * 7,
         out_specs=[hbm] * 4,
         scratch_shapes=[
             pltpu.VMEM((TOK, nctx * CH), BF),
@@ -723,6 +734,7 @@
             pltpu.VMEM((33, 256, 256), BF),
             pltpu.VMEM((33, 256, 256), BF),
             pltpu.VMEM((4, 128, 128), F32),
+            pltpu.VMEM((6, 128, 128), F32),
             pltpu.VMEM(spec, F32),
             pltpu.VMEM(spec, F32),
             pltpu.VMEM(spec, F32),
@@ -751,18 +763,40 @@
         compiler_params=pltpu.CompilerParams(
             collective_id=0, has_side_effects=True, vmem_limit_bytes=60 << 20
         ),
-    )(keys, values, queries, up, filters, w, *tables)
+    )(keys, values, queries, up, filters, w, tables)
+
+
+def finish_kernel(gq_ref, back_ref, key_ref, value_ref, fg_ref, gw_ref, gq_out, gk_out, gv_out, fg_out, gw_out):
+    gq_out[...] = gq_ref[...]
+    back = back_ref[...].astype(F32)
+    gk_out[...] = (back * value_ref[...].astype(F32)).astype(BF)
+    gv_out[...] = (back * key_ref[...].astype(F32)).astype(BF)
+    fg_out[...] = fg_ref[...].astype(F32)
+    gw_out[...] = gw_ref[...].astype(F32)
+
+
+def finish_call(gq, back, keys, values, fg, gw):
+    steps = FINISH_STEPS
+    by_rows = pl.BlockSpec((gq.shape[0] // steps, gq.shape[1]), lambda i: (i, 0))
+    by_cols = [pl.BlockSpec((a.shape[0], a.shape[1] // steps), lambda i: (0, i)) for a in (fg, gw)]
+    rows = jax.ShapeDtypeStruct(gq.shape, BF)
+    return pl.pallas_call(
+        finish_kernel,
+        name="finish",
+        grid=(steps,),
+        out_shape=[rows] * 3 + [jax.ShapeDtypeStruct(a.shape, F32) for a in (fg, gw)],
+        in_specs=[by_rows] * 4 + by_cols,
+        out_specs=[by_rows] * 3 + by_cols,
+        compiler_params=pltpu.CompilerParams(vmem_limit_bytes=60 << 20),
+    )(gq, back, keys, values, fg, gw)
 
 
 def per_device(queries, keys, values, upstream, filters, out_weight):
-    key_rows, value_rows = keys[0], values[0]
     gq, back, fg, gw = mixer_call(
-        key_rows, value_rows, queries[0], upstream[0], filters, out_weight
+        keys[0], values[0], queries[0], upstream[0], filters, out_weight
     )
-    back_wide = back.astype(F32)
-    grad_keys = (back_wide * value_rows.astype(F32)).astype(BF)
-    grad_values = (back_wide * key_rows.astype(F32)).astype(BF)
-    return (gq[None], grad_keys[None], grad_values[None], fg.astype(F32), gw.astype(F32))
+    gq, gk, gv, fg, gw = finish_call(gq, back, keys[0], values[0], fg, gw)
+    return gq[None], gk[None], gv[None], fg, gw
 
 
 def solution(mesh):

time: 92.4 us -> 86.2 us (0.933)
  other arithmetic: 4.25 us -> 0 us
  local copies, waits for them, and re-layouts: 1.21 us -> 0 us
    pallas_call x1, Pallas kernels: 86 us -> 82.4 us  [mixer_call(): pl.pallas_call(mixer_kernel, name='mixer', out_shape=[jax.ShapeDtypeStruc...]
    pallas_call x0 -> x1, Pallas kernels: none -> 3.05 us  [finish_call(): pl.pallas_call(finish_kernel, name='finish', grid=(steps,), out_shape=[ro...]
    broadcast_in_dim x1 -> x0, other arithmetic: 2.38 us -> none  [per_device(): grad_values[None]]
    convert_element_type x2 -> x0, other arithmetic: 1.87 us -> none  [the longest x1 1.04 us: per_device(): fg.astype(F32)]
    unnamed x11 -> x0, local copies, waits for them, and re-layouts: 1.21 us -> none
where the time goes in v2:
time: 86.2 us; the launch traced here: 86.1 us
  Pallas kernels  85.4 us (99%)
    pallas_call x1, Pallas kernels, mixer_call(): pl.pallas_call(mixer_kernel, name='mixer', out_shape=[jax.ShapeDtypeStruc...  82.4 us
    pallas_call x1, Pallas kernels, finish_call(): pl.pallas_call(finish_kernel, name='finish', grid=(steps,), out_shape=[ro...  3.05 us

profile of v2, /device:TPU:1, one launch (start us, length us, event | category | flops | bytes accessed | tf_op | source)
XLA Modules:
  0.0 86.1 jit_solution(14991216952298093828)
XLA Ops:
  0.6 82.4 %mixer.1 = (bf16[128,2048]{1,0:T(8,128)(2,1)}, bf16[128,2048]{1,0:T(8,128)(2,1)}, bf16[64,4096]{1,0:T(8,128)(2,1)}, bf16[64,2048]{1,0:T(8,128)(2,1)}) custom-call(bf16[128,2048]{1,0:T(8,128)(2,1)} %bitcast.7, bf16[128,2048]{1,0:T(8,128)(2,1)} %bitcast.9, bf16[128,2048]{1,0:T(8,128)(2,1)} %bitcast.11, bf16[128,2048]{1,0:T(8,128)(2,1)} %bitcast.12, ...), custom_call_target="tpu_custom_call" | custom-call | tf_op jit(solution)/shard_map/mixer/pallas_call | solution.py:709
  83.0 3.0 %finish.1 = (bf16[128,2048]{1,0:T(8,128)(2,1)}, bf16[128,2048]{1,0:T(8,128)(2,1)}, bf16[128,2048]{1,0:T(8,128)(2,1)}, f32[64,4096]{1,0:T(8,128)}, f32[64,2048]{1,0:T(8,128)}) custom-call(bf16[128,2048]{1,0:T(8,128)(2,1)} %get-tuple-element.14.gq_ref, bf16[128,2048]{1,0:T(8,128)(2,1)} %get-tuple-element.15.back_ref, bf16[128,2048]{1,0:T(8,128)(2,1)} %bitcast.8, ...), custom_call_target="tpu_custom_call" | custom-call | tf_op jit(solution)/shard_map/finish/pallas_call | solution.py:783

commit v3 on v2

--- a/solution.py
+++ b/solution.py
@@ -215,7 +215,7 @@
         mix_t[2 * j + 1] = turned[CH : 2 * CH]
         return carry
 
-    lax.fori_loop(0, nctx // 2, mix_block, 0)
+    lax.fori_loop(0, nctx // 2, mix_block, 0, unroll=4)
     mix_all[ctx] = mix_t[ctx]
     pl.semaphore_wait(barrier, len(peers))
 
@@ -255,29 +255,6 @@
             us[step, h].start()
     pair = send(up_ref, up_all.at[near], p_send.at[0], p_recv.at[0], dp, partner)
     pair.start()
-
-    loads[2].wait()
-
-    def query_block(j, carry):
-        cols = pl.ds(pl.multiple_of(j * 2 * CH, 2 * CH), 2 * CH)
-        turned = q_own[:, cols].astype(F32).T.astype(BF)
-        first = 2 * j
-        q_t[lax.rem(first, nnear), first // nnear] = turned[0:CH]
-        q_t[lax.rem(first + 1, nnear), (first + 1) // nnear] = turned[CH : 2 * CH]
-        return carry
-
-    lax.fori_loop(0, nctx // 2, query_block, 0)
-    qs = {}
-    for dy in sorted(range(NY), key=lambda a: min(a, NY - a)):
-        for dc in range(NC):
-            if dy or dc:
-                to = slot_of(dy, dc)
-                s = dy * NC + dc
-                qs[dy, dc] = send(
-                    q_t.at[to], q_all.at[near], q_send.at[0], q_recv.at[s], dp, zh * nnear + to
-                )
-                qs[dy, dc].start()
-    q_all[near] = q_t[near]
 
     scale = 2.0 / 8192
     loads[6].wait()
@@ -357,6 +334,29 @@
         return carry
 
     lax.fori_loop(0, 33, filter_step, 0, unroll=UNROLL)
+
+    loads[2].wait()
+
+    def query_block(j, carry):
+        cols = pl.ds(pl.multiple_of(j * 2 * CH, 2 * CH), 2 * CH)
+        turned = q_own[:, cols].astype(F32).T.astype(BF)
+        first = 2 * j
+        q_t[lax.rem(first, nnear), first // nnear] = turned[0:CH]
+        q_t[lax.rem(first + 1, nnear), (first + 1) // nnear] = turned[CH : 2 * CH]
+        return carry
+
+    lax.fori_loop(0, nctx // 2, query_block, 0, unroll=4)
+    qs = {}
+    for dy in sorted(range(NY), key=lambda a: min(a, NY - a)):
+        for dc in range(NC):
+            if dy or dc:
+                to = slot_of(dy, dc)
+                s = dy * NC + dc
+                qs[dy, dc] = send(
+                    q_t.at[to], q_all.at[near], q_send.at[0], q_recv.at[s], dp, zh * nnear + to
+                )
+                qs[dy, dc].start()
+    q_all[near] = q_t[near]
 
     rs = []
     if NY == 4:
@@ -546,7 +546,7 @@
                     b_send.at[0], b_recv.at[0], dp, to,
                 )
             )
-            if g == 0:
+            if g == 0 or s > nctx - nnear:
                 bs[g][-1].start()
 
     back_group(0)
@@ -609,7 +609,7 @@
         own.start()
         return own
 
-    for copy in bs[1]:
+    for copy in bs[1][: nctx - nnear]:
         copy.start()
     own_wa = [spread(zl, 0)]
     for copy in fzs:
@@ -637,7 +637,7 @@
         q_own[:, cols] = block.astype(F32).T.astype(BF)
         return carry
 
-    lax.fori_loop(0, nctx // 2, query_rows, 0)
+    lax.fori_loop(0, nctx // 2, query_rows, 0, unroll=4)
     out_q = pltpu.make_async_copy(q_own, gq_out, local.at[7])
     out_q.start()
     if NZL > 1:
@@ -651,7 +651,7 @@
         k_own[:, cols] = block.astype(F32).T.astype(BF)
         return carry
 
-    lax.fori_loop(0, nctx // 2, back_rows, 0)
+    lax.fori_loop(0, nctx // 2, back_rows, 0, unroll=4)
     out_b = pltpu.make_async_copy(k_own, back_out, local.at[8])
     out_b.start()
     for copy in [out_q, out_b, own_fa] + own_wa:

time: 86.2 us -> 84.5 us (0.980)
  Pallas kernels: 85.4 us -> 83.8 us
    pallas_call x1, Pallas kernels: 82.4 us -> 80.7 us  [mixer_call(): pl.pallas_call(mixer_kernel, name='mixer', out_shape=[jax.ShapeDtypeStruc...]
where the time goes in v3:
time: 84.5 us; the launch traced here: 84.4 us
  Pallas kernels  83.8 us (99%)
    pallas_call x1, Pallas kernels, mixer_call(): pl.pallas_call(mixer_kernel, name='mixer', out_shape=[jax.ShapeDtypeStruc...  80.7 us
    pallas_call x1, Pallas kernels, finish_call(): pl.pallas_call(finish_kernel, name='finish', grid=(steps,), out_shape=[ro...  3.05 us

profile of v3, /device:TPU:1, one launch (start us, length us, event | category | flops | bytes accessed | tf_op | source)
XLA Modules:
  0.0 84.4 jit_solution(10020070328351394294)
XLA Ops:
  0.6 80.7 %mixer.1 = (bf16[128,2048]{1,0:T(8,128)(2,1)}, bf16[128,2048]{1,0:T(8,128)(2,1)}, bf16[64,4096]{1,0:T(8,128)(2,1)}, bf16[64,2048]{1,0:T(8,128)(2,1)}) custom-call(bf16[128,2048]{1,0:T(8,128)(2,1)} %bitcast.7, bf16[128,2048]{1,0:T(8,128)(2,1)} %bitcast.9, bf16[128,2048]{1,0:T(8,128)(2,1)} %bitcast.11, bf16[128,2048]{1,0:T(8,128)(2,1)} %bitcast.12, ...), custom_call_target="tpu_custom_call" | custom-call | tf_op jit(solution)/shard_map/mixer/pallas_call | solution.py:709
  81.4 3.0 %finish.1 = (bf16[128,2048]{1,0:T(8,128)(2,1)}, bf16[128,2048]{1,0:T(8,128)(2,1)}, bf16[128,2048]{1,0:T(8,128)(2,1)}, f32[64,4096]{1,0:T(8,128)}, f32[64,2048]{1,0:T(8,128)}) custom-call(bf16[128,2048]{1,0:T(8,128)(2,1)} %get-tuple-element.14.gq_ref, bf16[128,2048]{1,0:T(8,128)(2,1)} %get-tuple-element.15.back_ref, bf16[128,2048]{1,0:T(8,128)(2,1)} %bitcast.8, ...), custom_call_target="tpu_custom_call" | custom-call | tf_op jit(solution)/shard_map/finish/pallas_call | solution.py:783

commit v4 on v3

--- a/solution.py
+++ b/solution.py
@@ -156,11 +156,11 @@
     gq_out, back_out, fg_out, gw_out,
     k_own, v_own, q_own, f_own, mix_t, q_t, mix_all, q_all, up_all, w_all, gg_all, sc_all, scl_all,
     ft, it, tab, wave, part, filt_s, mix_s, iq, conv_own, conv_all, back_own, fg_own, gate, gq_all, gq_in, back_in,
-    fg_x, fg_half, fg_z, fg_fin, gw_part, gw_x, gw_mid, gw_z, gw_fin, gw_sum,
+    fg_x, fg_half, fg_z, fg_fin, gw_part, gw_hop, gw_x, gw_mid, gw_z, gw_fin, gw_sum,
     m_send, m_recv, u_send, u_recv, r_send, r_recv, p_send, p_recv, q_send, q_recv,
     w_send, w_recv, v_send, v_recv, s_send, s_recv, c_send, c_recv, b_send, b_recv,
     fx_send, fx_recv, fz_send, fz_recv, fa_send, fa_recv,
-    g_send, g_recv, wx_send, wx_recv, wz_send, wz_recv, wa_send, wa_recv, local,
+    g_send, g_recv, wx_send, wx_recv, hop_recv, wz_send, wz_recv, wa_send, wa_recv, local,
 ):
     at = place()
     dp, ctx, near, zh, zl, x = (at[k] for k in ("dp", "ctx", "near", "zh", "zl", "x"))
@@ -482,18 +482,31 @@
             gate[h * CH : (h + 1) * CH, i * TOK : (i + 1) * TOK] = (
                 q_all[i, h].astype(F32) * conv
             ).astype(BF)
-    wxs = []
-    for s in list(range(1, NX)) + [0]:
-        to = lax.rem(x + s, NX)
+    crowd = NZH * CH
+    low, high = pl.ds(0, crowd // 2), pl.ds(crowd // 2, crowd // 2)
+    right, left = lax.rem(x + 1, NX), lax.rem(x + NX - 1, NX)
+
+    def tile(to):
         cols = pl.ds(pl.multiple_of(to * wide, wide), wide)
         up = up_all[:, :, cols].reshape(nnear * TOK, wide)
         gw_part[to] = jnp.dot(gate[...], up, preferred_element_type=F32).astype(BF)
-        if s:
-            wxs.append(
-                send(gw_part.at[to], gw_x.at[x], wx_send.at[0], wx_recv.at[0], zl * NX + to, ctx)
-            )
-            wxs[-1].start()
-    gw_x[x] = gw_part[x]
+
+    def pass_on(to, src, dst, hop, i):
+        copy = send(src, dst, wx_send.at[0], (hop_recv if hop else wx_recv).at[i], zl * NX + to, ctx)
+        copy.start()
+        return copy
+
+    far_x = lax.rem(x + 2, NX)
+    tile(far_x)
+    hops = [
+        pass_on(right, gw_part.at[far_x, low], gw_hop.at[0], True, 0),
+        pass_on(left, gw_part.at[far_x, high], gw_hop.at[1], True, 1),
+    ]
+    tile(right)
+    pass_on(right, gw_part.at[right, high], gw_x.at[0, high], False, 0)
+    tile(left)
+    pass_on(left, gw_part.at[left, low], gw_x.at[1, low], False, 0)
+    tile(x)
     gs = []
     for s in range(1, nnear):
         to = lax.rem(near + s, nnear)
@@ -504,6 +517,12 @@
     for h in range(NZH):
         gq_in[h, near] = gq_all[near, h]
 
+    hops[0].wait_recv()
+    gw_part[right, low] = (gw_part[right, low].astype(F32) + gw_hop[0].astype(F32)).astype(BF)
+    pass_on(right, gw_part.at[right, low], gw_x.at[0, low], False, 0)
+    hops[1].wait_recv()
+    gw_part[left, high] = (gw_part[left, high].astype(F32) + gw_hop[1].astype(F32)).astype(BF)
+    pass_on(left, gw_part.at[left, high], gw_x.at[1, high], False, 0)
     bs, fxs = [[], []], []
     lanes = seq // NX
 
@@ -553,12 +572,10 @@
     back_group(1)
     back_in[ctx] = back_own[ctx]
     fg_x[x] = fg_own[:, pl.ds(pl.multiple_of(x * lanes, lanes), lanes)]
-    if NX > 1:
-        drain(gw_x.at[pl.ds(0, NX - 1)], wx_recv.at[0])
+    drain(gw_x, wx_recv.at[0])
     for h in range(NZH):
-        total = gw_x[0, h * CH : (h + 1) * CH].astype(F32)
-        for i in range(1, NX):
-            total = total + gw_x[i, h * CH : (h + 1) * CH].astype(F32)
+        band = slice(h * CH, (h + 1) * CH)
+        total = gw_part[x, band].astype(F32) + gw_x[0, band].astype(F32) + gw_x[1, band].astype(F32)
         for i in range(NZL):
             gw_mid[h, i] = total[:, i * narrow : (i + 1) * narrow].astype(BF)
     zs = []
@@ -588,6 +605,8 @@
         fzs.append(send(fg_half, fg_z.at[zl], fz_send.at[s], fz_recv.at[s], to * NX + x, ctx))
         fzs[-1].start()
     fg_z[zl] = fg_half[...]
+    for copy in bs[1][:nnear]:
+        copy.start()
     drain(gw_z.at[pl.ds(0, nz - 1)], wz_recv.at[0])
     total = gw_z[0].astype(F32)
     for i in range(1, nz):
@@ -609,7 +628,7 @@
         own.start()
         return own
 
-    for copy in bs[1][: nctx - nnear]:
+    for copy in bs[1][nnear : nctx - nnear]:
         copy.start()
     own_wa = [spread(zl, 0)]
     for copy in fzs:
@@ -678,9 +697,9 @@
     drain(gw_z.at[pl.ds(0, nz - 1)], wz_send.at[0])
     if NX > 1:
         drain(fg_x.at[pl.ds(0, NX - 1)], fx_send.at[0])
-        drain(gw_x.at[pl.ds(0, NX - 1)], wx_send.at[0])
+        drain(gw_part.at[pl.ds(0, 3)], wx_send.at[0])
         drain(fg_x.at[pl.ds(0, NX - 1)], fa_send.at[0])
-        gw_bytes = gw_x.at[pl.ds(0, NX - 1), pl.ds(0, CH), pl.ds(0, NZL * narrow)]
+        gw_bytes = gw_part.at[pl.ds(0, NX - 1), pl.ds(0, CH), pl.ds(0, NZL * narrow)]
         drain(gw_bytes, wa_send.at[0])
         drain(gw_bytes, wa_recv.at[0])
         drain(fg_x.at[pl.ds(0, NX - 1)], fa_recv.at[0])
@@ -704,7 +723,7 @@
     spec = (33, CH, 256)
     sems = [
         2, 2, 1, 4, 1, 2, 1, 4, 1, nnear, 1, NZH, 1, 1, 2, 2, 1, 1, 1, 1,
-        1, 1, NZL, NZL, 1, 1, 1, 1, 1, 1, 2, 2, 1, 1,
+        1, 1, NZL, NZL, 1, 1, 1, 1, 1, 1, 2, 2, 2, 1, 1,
     ]
     return pl.pallas_call(
         mixer_kernel,
@@ -752,7 +771,8 @@
             pltpu.VMEM((NZL, CH, seq // NX), BF),
             pltpu.VMEM((CH, seq // NX), BF),
             pltpu.VMEM((NX, NZH * CH, wide), BF),
-            pltpu.VMEM((NX, NZH * CH, wide), BF),
+            pltpu.VMEM((2, NZH * CH // 2, wide), BF),
+            pltpu.VMEM((2, NZH * CH, wide), BF),
             pltpu.VMEM((NZH, NZL, CH, narrow), BF),
             pltpu.VMEM((nz, CH, narrow), BF),
             pltpu.VMEM((CH, narrow), BF),

time: 84.5 us -> 84.5 us (level)
  no operation moved by 1% of the time
where the time goes in v4:
time: 84.5 us; the launch traced here: 84.4 us
  Pallas kernels  83.7 us (99%)
    pallas_call x1, Pallas kernels, mixer_call(): pl.pallas_call(mixer_kernel, name='mixer', out_shape=[jax.ShapeDtypeStruc...  80.7 us
    pallas_call x1, Pallas kernels, finish_call(): pl.pallas_call(finish_kernel, name='finish', grid=(steps,), out_shape=[ro...  3.05 us

profile of v4, /device:TPU:1, one launch (start us, length us, event | category | flops | bytes accessed | tf_op | source)
XLA Modules:
  0.0 84.4 jit_solution(9419890691532434354)
XLA Ops:
  0.6 80.7 %mixer.1 = (bf16[128,2048]{1,0:T(8,128)(2,1)}, bf16[128,2048]{1,0:T(8,128)(2,1)}, bf16[64,4096]{1,0:T(8,128)(2,1)}, bf16[64,2048]{1,0:T(8,128)(2,1)}) custom-call(bf16[128,2048]{1,0:T(8,128)(2,1)} %bitcast.7, bf16[128,2048]{1,0:T(8,128)(2,1)} %bitcast.9, bf16[128,2048]{1,0:T(8,128)(2,1)} %bitcast.11, bf16[128,2048]{1,0:T(8,128)(2,1)} %bitcast.12, ...), custom_call_target="tpu_custom_call" | custom-call | tf_op jit(solution)/shard_map/mixer/pallas_call | solution.py:728
  81.3 3.0 %finish.1 = (bf16[128,2048]{1,0:T(8,128)(2,1)}, bf16[128,2048]{1,0:T(8,128)(2,1)}, bf16[128,2048]{1,0:T(8,128)(2,1)}, f32[64,4096]{1,0:T(8,128)}, f32[64,2048]{1,0:T(8,128)}) custom-call(bf16[128,2048]{1,0:T(8,128)(2,1)} %get-tuple-element.14.gq_ref, bf16[128,2048]{1,0:T(8,128)(2,1)} %get-tuple-element.15.back_ref, bf16[128,2048]{1,0:T(8,128)(2,1)} %bitcast.8, ...), custom_call_target="tpu_custom_call" | custom-call | tf_op jit(solution)/shard_map/finish/pallas_call | solution.py:803
